TPU v7x, 256 devices: a whole 4x4x8 slice. The times are simulated.
256 devices in a mesh: mem: 32 (over x, y, core), lat: 8 (over z).
Axes of the slice: x: 4, y: 4, z: 8, core: 2. Of those that a mesh axis runs over, the one named last changes fastest.
Arguments:
- perturb: bfloat16 [128, 4, 256, 1024], P('mem', None, 'lat'), may hold values from -16 to 16
- gradient: float32 [4, 256, 1024], P(None, 'lat', 'mem'), may hold values from -6 to 6
- k_north: float32 [4, 256, 1024], P(None, 'lat'), may hold values from 0.1 to 0.35
- k_east: float32 [4, 256, 1024], P(None, 'lat'), may hold values from 0.02 to 0.15
- scale: float32 [4, 256, 1024], P(None, 'lat'), may hold values from 0.25 to 1
Outputs:
- product: float32 [4, 256, 1024], P(None, 'lat', 'mem')
All inputs are finite; a program needn't handle non-finite values.
Results may differ from a plain program's by a relative error of at most 0.0003.
Values sent between devices are 32-bit elements; how exact they have to be, the bound alone decides.
No kernel may reach another device: no remote copies, remote signals or barrier semaphores. Data moves between devices by JAX's collectives and lax.ppermute only.
A program may use at most 128 MiB of HBM per device.

v0:
```python
import jax
import jax.numpy as jnp
from jax import lax
from jax.sharding import Mesh
from jax.sharding import PartitionSpec as P

SWEEP = 4
MEM = ("mem_0", "mem_1", "mem_2")


def in_order(parts, dim):
    parts = jnp.moveaxis(parts, 0, dim)
    lengths = parts.shape
    return parts.reshape(*lengths[:dim], lengths[dim] * lengths[dim + 1], *lengths[dim + 2 :])


def all_blocks(array, axes, sequence):
    parts = array
    for k in sequence:
        parts = lax.all_gather(parts, axes[k])
    done = sequence[::-1]
    back = [done.index(k) for k in range(len(axes))]
    parts = parts.transpose(*back, *range(len(axes), parts.ndim))
    return parts.reshape(-1, *array.shape)


def whole_of(array, axes, sequence, dim):
    return in_order(all_blocks(array, axes, sequence), dim)


def with_halo(array, sides, width):
    for axis, dim in sides:
        size, length = (lax.axis_size(axis), array.shape[dim])
        up = [(i, (i + 1) % size) for i in range(size - 1)]
        down = [(j, i) for i, j in up]
        last = lax.slice_in_dim(array, length - width, length, axis=dim)
        leading = lax.slice_in_dim(array, 0, width, axis=dim)
        before = lax.ppermute(last, axis, up)
        after = lax.ppermute(leading, axis, down)
        array = jnp.concatenate([before, array, after], axis=dim)
    return array


def cut_along(array, dim, length):
    lengths = array.shape
    parts = array.reshape(*lengths[:dim], length, lengths[dim] // length, *lengths[dim + 1 :])
    return jnp.moveaxis(parts, dim, 0)


def sent_and_summed(array, axis, dim):
    length = lax.axis_size(axis)
    parts = lax.all_to_all(cut_along(array, dim, length), axis, 0, 0, tiled=True)
    return jnp.sum(parts, axis=0)


def spread(values, k_north, k_east):
    middle = values[..., 1:-1, :]
    north_flux = k_north[:, 1:-1] * (values[..., 2:, :] - middle)
    south_flux = k_north[:, :-2] * (middle - values[..., :-2, :])
    east_face = k_east[:, 1:-1]
    east_flux = east_face * (jnp.roll(middle, -1, -1) - middle) - jnp.roll(east_face, 1, -1) * (
        middle - jnp.roll(middle, 1, -1)
    )
    return north_flux - south_flux + east_flux


def adjoint_step(values, coefficients):
    return values[..., 1:-1, :] + spread(coefficients[2] * values, coefficients[0], coefficients[1])


def forward_step(values, coefficients):
    return values[..., 1:-1, :] + coefficients[2][:, 1:-1] * spread(
        values, coefficients[0], coefficients[1]
    )


def shards(perturb, gradient, k_north, k_east, scale):
    member_count = perturb.shape[0]
    row_count = perturb.shape[2]
    row_start = lax.axis_index("lat") * row_count
    global_rows = row_start + jnp.arange(row_count, dtype=jnp.int32)
    top_row = global_rows == lax.axis_size("lat") * row_count - 1
    masked_north = jnp.where(top_row[None, :, None], jnp.float32(0.0), k_north)
    field = (
        perturb.astype(jnp.float32)
        * whole_of(gradient, (("mem_0", "mem_1"), "mem_2"), (0, 1), 2)[None]
    )
    halo_depth = SWEEP
    stacked = jnp.stack([masked_north, k_east, scale])
    padded_coef = with_halo(stacked, (("lat", 2),), halo_depth)
    for stepper in (adjoint_step, forward_step):
        values = with_halo(field, (("lat", 2),), SWEEP)
        for section in range(SWEEP):
            row_span = row_count + 2 * (SWEEP - section)
            values = stepper(
                values, lax.slice_in_dim(padded_coef, section, section + row_span, axis=2)
            )
        field = values
    member_terms = jnp.sum(perturb.astype(jnp.float32) * field, axis=0)
    summed = sent_and_summed(member_terms, MEM, 2)
    return summed / jnp.float32(member_count * lax.axis_size(MEM) - 1)


def solution(mesh):
    torus = Mesh(
        mesh.devices.reshape(4, 4, 2, mesh.shape["lat"]), ("mem_0", "mem_1", "mem_2", "lat")
    )
    in_specs = (
        P(MEM, None, "lat", None),
        P(None, "lat", MEM),
        P(None, "lat", None),
        P(None, "lat", None),
        P(None, "lat", None),
    )
    out_specs = P(None, "lat", MEM)
    return jax.shard_map(
        shards, mesh=torus, in_specs=in_specs, out_specs=out_specs, check_vma=False
    )
```

profile of v0, /device:TPU:1, one launch (start us, length us, event | category | flops | bytes accessed | tf_op | source)
XLA Modules:
  0.0 129.9 jit_solution(7912672980908324119)
XLA Ops:
  0.0 1.2 select_bitcast_fusion
  1.2 1.9 %pad_maximum_fusion.13 = (f32[3,4,4,1024]{3,2,1,0:T(4,128)}, f32[3,4,4,1024]{3,2,1,0:T(4,128)S(1)}) fusion(f32[1,4,32,1024]{3,2,1,0:T(8,128)} %bitcast.42, f32[1,4,32,1024]{3,2,1,0:T(8,128)} %bitcast.44, f32[1,4,32,1024]{3,2,1,0:T(8,128)S(1)} %select_bitcast_fusion), kind=kLoop, calls=%fused_computation.135 | loop fusion | flops 196608 | bytes 1966080 | tf_op jit(solution)/shard_map/slice | solution.py:36
  3.1 4.4 %collective-permute-start.2 = (f32[3,4,4,1024]{3,2,1,0:T(4,128)}, f32[3,4,4,1024]{3,2,1,0:T(4,128)S(1)}, u32[]{:S(2)}, u32[]{:S(2)}) collective-permute-start(f32[3,4,4,1024]{3,2,1,0:T(4,128)} %get-tuple-element.59), channel_id=1, source_target_pairs={{0,1},{1,2},{2,3},{3,4},{4,5},{5,6},{6,7},{8,9},{9,10},{10,11},{11... | collective-permute-start | bytes 589832 | tf_op jit(solution)/shard_map/ppermute | solution.py:38
  7.4 1.3 collective-permute-start.3
  8.7 19.8 %all-gather = f32[64,32,32]{2,1,0:T(8,128)S(1)} all-gather(f32[4,32,32]{2,1,0:T(8,128)S(1)} %copy-done.3), channel_id=2, replica_groups=mesh['mem_0'=4,'mem_1'=4,'mem_2'=2,'lat'=8] {'mem_0','mem_1'}, dimensions={0}, use_global_device_ids=true | all-gather | bytes 278528 | tf_op jit(solution)/shard_map/all_gather | solution.py:20
  28.6 9.3 %all-gather.1 = f32[32,4,32,32]{3,2,1,0:T(8,128)S(1)} all-gather(f32[16,4,32,32]{3,2,1,0:T(8,128)S(1)} %bitcast.41), channel_id=3, replica_groups=mesh['mem_0'=4,'mem_1'=4,'mem_2'=2,'lat'=8] {'mem_2'}, dimensions={0}, use_global_device_ids=true | all-gather | bytes 786432 | tf_op jit(solution)/shard_map/all_gather | solution.py:20
  38.1 1.2 copy.11
  39.4 1.0 mul.146
  40.3 1.6 %convert_multiply_fusion.1 = f32[4,4,32,1024]{3,2,1,0:T(8,128)S(1)} fusion(bf16[4,4,32,1024]{3,2,1,0:T(8,128)(2,1)} %param.5, f32[4,32,1024]{2,1,0:T(8,128)S(1)} %mul.146), kind=kLoop, calls=%fused_computation.1 | loop fusion | flops 1048576 | bytes 3670016 | tf_op jit(solution)/shard_map/mul | solution.py:85
  42.0 4.3 %collective-permute-start = (f32[4,4,4,1024]{3,2,1,0:T(4,128)S(1)}, f32[4,4,4,1024]{3,2,1,0:T(4,128)S(1)}, u32[]{:S(2)}, u32[]{:S(2)}) collective-permute-start(f32[4,4,4,1024]{3,2,1,0:T(4,128)S(1)} %get-tuple-element.45), channel_id=1, source_target_pairs={{0,1},{1,2},{2,3},{3,4},{4,5},{5,6},{6,7},{8,9},{9,10},{10,11},{11... | collective-permute-start | bytes 786440 | tf_op jit(solution)/shard_map/ppermute | solution.py:38
  46.3 1.3 collective-permute-start.1
  47.7 1.2 pad_maximum_fusion.6
  49.4 0.3 slice_bitcast_fusion.8
  50.0 0.3 slice_bitcast_fusion.5
  50.5 0.3 slice_bitcast_fusion.2
  51.4 0.3 fusion.95
  51.7 0.3 fusion.94
  52.2 3.5 %collective-permute-done.1 = f32[4,4,4,1024]{3,2,1,0:T(4,128)S(1)} collective-permute-done((f32[4,4,4,1024]{3,2,1,0:T(4,128)S(1)}, f32[4,4,4,1024]{3,2,1,0:T(4,128)S(1)}, u32[]{:S(2)}, u32[]{:S(2)}) %collective-permute-start.1) | collective-permute-done | bytes 262176 | tf_op jit(solution)/shard_map/ppermute | solution.py:39
  55.8 0.8 pad_maximum_fusion.4
  56.6 1.4 %fusion.89 = (f32[4,4,38,1023]{3,2,1,0:T(8,128)S(1)}, f32[4,4,38,1023]{3,2,1,0:T(8,128)S(1)}) fusion(f32[4,4,40,1024]{3,2,1,0:T(8,128)S(1)} %get-tuple-element.38), kind=kLoop, calls=%fused_computation.151 | loop fusion | bytes 9951744 | tf_op jit(solution)/shard_map/jit(_roll_static)/slice | solution.py:61
  58.2 2.7 %broadcast_multiply_fusion.2 = (f32[4,4,38,1024]{3,2,1,0:T(8,128)S(1)}, f32[4,4,38,1024]{3,2,1,0:T(8,128)S(1)}) fusion(f32[4,38,1024]{2,1,0:T(8,128)S(1)} %get-tuple-element.55, f32[4,4,38,1023]{3,2,1,0:T(8,128)S(1)} %get-tuple-element.40, f32[4,4,38,1]{3,2,1,0:T(8,128)S(1)} %get-tuple-element.42, f32[4,38,1024]{2,1,0:T(8,128)S(1)} %get-tuple-element.69, ...), kind=kLoop, calls=%fused_computation.114 | loop fusion | flops 9338880 | bytes 23035904 | tf_op jit(solution)/shard_map/mul | solution.py:68
  60.8 1.4 %fusion.87 = (f32[4,4,36,1023]{3,2,1,0:T(8,128)S(1)}, f32[4,4,36,1023]{3,2,1,0:T(8,128)S(1)}) fusion(f32[4,4,38,1024]{3,2,1,0:T(8,128)S(1)} %get-tuple-element.9), kind=kLoop, calls=%fused_computation.149 | loop fusion | bytes 9427968 | tf_op jit(solution)/shard_map/jit(_roll_static)/slice | solution.py:61
  62.4 2.5 %broadcast_multiply_fusion.1 = (f32[4,4,36,1024]{3,2,1,0:T(8,128)S(1)}, f32[4,4,36,1024]{3,2,1,0:T(8,128)S(1)}) fusion(f32[4,36,1024]{2,1,0:T(8,128)S(1)} %get-tuple-element.52, f32[4,4,36,1023]{3,2,1,0:T(8,128)S(1)} %get-tuple-element.34, f32[4,4,36,1]{3,2,1,0:T(8,128)S(1)} %get-tuple-element.36, f32[4,36,1024]{2,1,0:T(8,128)S(1)} %get-tuple-element.70, ...), kind=kLoop, calls=%fused_computation.113 | loop fusion | flops 8847360 | bytes 21823488 | tf_op jit(solution)/shard_map/mul | solution.py:68
  65.0 1.4 %fusion.85 = (f32[4,4,34,1023]{3,2,1,0:T(8,128)S(1)}, f32[4,4,34,1023]{3,2,1,0:T(8,128)S(1)}) fusion(f32[4,4,36,1024]{3,2,1,0:T(8,128)S(1)} %get-tuple-element.7), kind=kLoop, calls=%fused_computation.147 | loop fusion | bytes 8904192 | tf_op jit(solution)/shard_map/jit(_roll_static)/slice | solution.py:61
  66.6 2.5 %broadcast_multiply_fusion = (f32[4,4,34,1024]{3,2,1,0:T(8,128)S(1)}, f32[4,4,34,1024]{3,2,1,0:T(8,128)S(1)}) fusion(f32[4,34,1024]{2,1,0:T(8,128)S(1)} %get-tuple-element.49, f32[4,4,34,1023]{3,2,1,0:T(8,128)S(1)} %get-tuple-element.30, f32[4,4,34,1]{3,2,1,0:T(8,128)S(1)} %get-tuple-element.32, f32[4,34,1024]{2,1,0:T(8,128)S(1)} %get-tuple-element.71, ...), kind=kLoop, calls=%fused_computation.112 | loop fusion | flops 8355840 | bytes 20611072 | tf_op jit(solution)/shard_map/mul | solution.py:68
  69.1 1.1 fusion.84
  70.3 1.8 %fusion.65 = f32[4,4,32,1024]{3,2,1,0:T(8,128)S(1)} fusion(f32[4,4,34,1024]{3,2,1,0:T(8,128)S(1)} %get-tuple-element.5, f32[4,4,34,1024]{3,2,1,0:T(8,128)S(1)} %get-tuple-element.6, f32[4,4,32,1]{3,2,1,0:T(8,128)S(1)} %get-tuple-element.26, f32[4,4,32,1023]{3,2,1,0:T(8,128)S(1)} %get-tuple-element.28, f32[4,4,32,1023]{3,2,1,0:T(8,128)S(1)} %get-tuple-element.27, ...), kind=kLoop, calls=%fused_computation.98 | loop fusion | flops 7340032 | bytes 16777216 | tf_op jit(solution)/shard_map/add | solution.py:68
  72.3 4.8 %collective-permute-start.4 = (f32[4,4,4,1024]{3,2,1,0:T(4,128)S(1)}, f32[4,4,4,1024]{3,2,1,0:T(4,128)S(1)}, u32[]{:S(2)}, u32[]{:S(2)}) collective-permute-start(f32[4,4,4,1024]{3,2,1,0:T(4,128)S(1)} %get-tuple-element.43), channel_id=1, source_target_pairs={{0,1},{1,2},{2,3},{3,4},{4,5},{5,6},{6,7},{8,9},{9,10},{10,11},{11... | collective-permute-start | bytes 786440 | tf_op jit(solution)/shard_map/ppermute | solution.py:38
  77.1 1.3 collective-permute-start.5
  78.7 2.8 %collective-permute-done.4 = f32[4,4,4,1024]{3,2,1,0:T(4,128)S(1)} collective-permute-done((f32[4,4,4,1024]{3,2,1,0:T(4,128)S(1)}, f32[4,4,4,1024]{3,2,1,0:T(4,128)S(1)}, u32[]{:S(2)}, u32[]{:S(2)}) %collective-permute-start.4) | collective-permute-done | bytes 262176 | tf_op jit(solution)/shard_map/ppermute | solution.py:38
  81.5 5.4 %collective-permute-done.5 = f32[4,4,4,1024]{3,2,1,0:T(4,128)S(1)} collective-permute-done((f32[4,4,4,1024]{3,2,1,0:T(4,128)S(1)}, f32[4,4,4,1024]{3,2,1,0:T(4,128)S(1)}, u32[]{:S(2)}, u32[]{:S(2)}) %collective-permute-start.5) | collective-permute-done | bytes 262176 | tf_op jit(solution)/shard_map/ppermute | solution.py:39
  86.9 0.6 pad_maximum_fusion.5
  87.5 1.4 %fusion.82 = (f32[4,4,38,1023]{3,2,1,0:T(8,128)S(1)}, f32[4,4,38,1023]{3,2,1,0:T(8,128)S(1)}) fusion(f32[4,4,40,1024]{3,2,1,0:T(8,128)S(1)} %pad_maximum_fusion.5), kind=kLoop, calls=%fused_computation.144 | loop fusion | bytes 9951744 | tf_op jit(solution)/shard_map/jit(_roll_static)/slice | solution.py:62
  88.9 2.7 %fusion.18 = f32[4,4,38,1024]{3,2,1,0:T(8,128)S(1)} fusion(f32[4,4,4,1024]{3,2,1,0:T(4,128)S(1)} %collective-permute-done.5, f32[4,4,32,1024]{3,2,1,0:T(8,128)S(1)} %fusion.65, f32[4,4,4,1024]{3,2,1,0:T(4,128)S(1)} %collective-permute-done.4, f32[4,4,40,1024]{3,2,1,0:T(8,128)S(1)} %pad_maximum_fusion.5, f32[4,4,38,1023]{3,2,1,0:T(8,128)S(1)} %get-tuple-element.24, ...), kind=kLoop, calls=%fused_computation.25 | loop fusion | flops 11829248 | bytes 20671744 | tf_op jit(solution)/shard_map/add | solution.py:72
  91.6 1.4 %fusion.81 = (f32[4,4,36,1023]{3,2,1,0:T(8,128)S(1)}, f32[4,4,36,1023]{3,2,1,0:T(8,128)S(1)}) fusion(f32[4,4,38,1024]{3,2,1,0:T(8,128)S(1)} %fusion.18), kind=kLoop, calls=%fused_computation.143 | loop fusion | bytes 9427968 | tf_op jit(solution)/shard_map/jit(_roll_static)/slice | solution.py:62
  93.2 2.1 %fusion.10 = f32[4,4,36,1024]{3,2,1,0:T(8,128)S(1)} fusion(f32[4,4,38,1024]{3,2,1,0:T(8,128)S(1)} %fusion.18, f32[4,4,36,1]{3,2,1,0:T(8,128)S(1)} %get-tuple-element.20, f32[4,4,36,1023]{3,2,1,0:T(8,128)S(1)} %get-tuple-element.22, f32[4,4,36,1023]{3,2,1,0:T(8,128)S(1)} %get-tuple-element.21, f32[4,4,36,1]{3,2,1,0:T(8,128)S(1)} %get-tuple-element.19, ...), kind=kLoop, calls=%fused_computation.15 | loop fusion | flops 8847360 | bytes 17104896 | tf_op jit(solution)/shard_map/add | solution.py:72
  95.3 1.2 fusion.79
  96.7 2.0 %fusion.4 = f32[4,4,34,1024]{3,2,1,0:T(8,128)S(1)} fusion(f32[4,4,36,1024]{3,2,1,0:T(8,128)S(1)} %fusion.10, f32[4,4,34,1]{3,2,1,0:T(8,128)S(1)} %get-tuple-element.16, f32[4,4,34,1023]{3,2,1,0:T(8,128)S(1)} %get-tuple-element.18, f32[4,4,34,1023]{3,2,1,0:T(8,128)S(1)} %get-tuple-element.17, f32[4,4,34,1]{3,2,1,0:T(8,128)S(1)} %get-tuple-element.15, ...), kind=kLoop, calls=%fused_computation.7 | loop fusion | flops 8355840 | bytes 16154624 | tf_op jit(solution)/shard_map/add | solution.py:72
  98.7 1.1 fusion.77
  100.0 1.9 %fusion.55 = f32[4,32,1024]{2,1,0:T(8,128)S(1)} fusion(bf16[4,4,32,1024]{3,2,1,0:T(8,128)(2,1)S(1)} %copy-done, f32[4,4,34,1024]{3,2,1,0:T(8,128)S(1)} %fusion.4, f32[4,4,32,1]{3,2,1,0:T(8,128)S(1)} %get-tuple-element.12, f32[4,4,32,1023]{3,2,1,0:T(8,128)S(1)} %get-tuple-element.14, f32[4,4,32,1023]{3,2,1,0:T(8,128)S(1)} %get-tuple-element.13, ...), kind=kLoop, calls=%fused_computation.85 | loop fusion | flops 9306112 | bytes 14680064 | tf_op jit(solution)/shard_map/reduce_sum | solution.py:99
  101.9 0.7 reshape.33
  102.6 2.6 %copy.12 = f32[32,4,32,32]{3,2,1,0:T(8,128)} copy(f32[32,4,32,32]{3,0,2,1:T(8,128)S(1)} %bitcast.38) | data formatting | bytes 1048576 | tf_op jit(solution)/shard_map/transpose | solution.py:47
  105.2 2.5 %reshape.36 = f32[32,1,4096]{2,1,0:T(1,128)S(1)} reshape(f32[32,4,32,32]{3,2,1,0:T(8,128)} %copy.12) | data formatting | bytes 1048576
  107.6 18.3 %all_to_all.5 = f32[32,1,4096]{2,1,0:T(1,128)S(1)} all-to-all(f32[32,1,4096]{2,1,0:T(1,128)S(1)} %reshape.36), channel_id=1, replica_groups=mesh['mem_0'=4,'mem_1'=4,'mem_2'=2,'lat'=8] {'mem_0','mem_1','mem_2'}, dimensions={0} | all-to-all | bytes 1048576 | tf_op jit(solution)/shard_map/all_to_all | solution.py:52
  125.9 0.5 broadcast.29
  126.5 1.9 %reduce = f32[32,4096]{1,0:T(8,128)S(1)} reduce(f32[32,1,4096]{2,1,0:T(1,128)S(1)} %all_to_all.5, f32[]{:T(128)} %broadcast.29), dimensions={1}, to_apply=%all_to_all.3.reduce_sub_computation | reduce | bytes 1048580 | tf_op jit(solution)/shard_map/all_to_all | solution.py:52
  128.4 0.7 reshape.37
  129.3 0.6 broadcast_multiply_fusion.4
  (42 shorter events, 3.7 us)
Async XLA Ops:
  0.0 8.7 %copy-start.3 = (f32[4,32,32]{2,1,0:T(8,128)S(1)}, f32[4,32,32]{2,1,0:T(8,128)}, u32[]{:S(2)}) copy-start(f32[4,32,32]{2,1,0:T(8,128)} %param.6) | copy-start | bytes 49156
  3.1 44.6 %collective-permute-start.2 = (f32[3,4,4,1024]{3,2,1,0:T(4,128)}, f32[3,4,4,1024]{3,2,1,0:T(4,128)S(1)}, u32[]{:S(2)}, u32[]{:S(2)}) collective-permute-start(f32[3,4,4,1024]{3,2,1,0:T(4,128)} %get-tuple-element.59), channel_id=1, source_target_pairs={{0,1},{1,2},{2,3},{3,4},{4,5},{5,6},{6,7},{8,9},{9,10},{10,11},{11... | collective-permute-start | bytes 589832 | tf_op jit(solution)/shard_map/ppermute | solution.py:38
  7.4 40.2 %collective-permute-start.3 = (f32[3,4,4,1024]{3,2,1,0:T(4,128)S(1)}, f32[3,4,4,1024]{3,2,1,0:T(4,128)}, u32[]{:S(2)}, u32[]{:S(2)}) collective-permute-start(f32[3,4,4,1024]{3,2,1,0:T(4,128)S(1)} %get-tuple-element.60), channel_id=1, source_target_pairs={{1,0},{2,1},{3,2},{4,3},{5,4},{6,5},{7,6},{9,8},{10,9},{11,10},{12... | collective-permute-start | bytes 589832 | tf_op jit(solution)/shard_map/ppermute | solution.py:39
  40.3 7.4 %copy-start.1 = (f32[4,32,1024]{2,1,0:T(8,128)S(1)}, f32[4,32,1024]{2,1,0:T(8,128)}, u32[]{:S(2)}) copy-start(f32[4,32,1024]{2,1,0:T(8,128)} %param.9) | copy-start | bytes 1572868
  40.3 7.4 %copy-start.2 = (f32[4,32,1024]{2,1,0:T(8,128)S(1)}, f32[4,32,1024]{2,1,0:T(8,128)}, u32[]{:S(2)}) copy-start(f32[4,32,1024]{2,1,0:T(8,128)} %param.8) | copy-start | bytes 1572868
  42.0 10.2 %collective-permute-start = (f32[4,4,4,1024]{3,2,1,0:T(4,128)S(1)}, f32[4,4,4,1024]{3,2,1,0:T(4,128)S(1)}, u32[]{:S(2)}, u32[]{:S(2)}) collective-permute-start(f32[4,4,4,1024]{3,2,1,0:T(4,128)S(1)} %get-tuple-element.45), channel_id=1, source_target_pairs={{0,1},{1,2},{2,3},{3,4},{4,5},{5,6},{6,7},{8,9},{9,10},{10,11},{11... | collective-permute-start | bytes 786440 | tf_op jit(solution)/shard_map/ppermute | solution.py:38
  46.3 9.4 %collective-permute-start.1 = (f32[4,4,4,1024]{3,2,1,0:T(4,128)S(1)}, f32[4,4,4,1024]{3,2,1,0:T(4,128)S(1)}, u32[]{:S(2)}, u32[]{:S(2)}) collective-permute-start(f32[4,4,4,1024]{3,2,1,0:T(4,128)S(1)} %get-tuple-element.46), channel_id=1, source_target_pairs={{1,0},{2,1},{3,2},{4,3},{5,4},{6,5},{7,6},{9,8},{10,9},{11,10},{12... | collective-permute-start | bytes 786440 | tf_op jit(solution)/shard_map/ppermute | solution.py:39
  72.3 9.2 %collective-permute-start.4 = (f32[4,4,4,1024]{3,2,1,0:T(4,128)S(1)}, f32[4,4,4,1024]{3,2,1,0:T(4,128)S(1)}, u32[]{:S(2)}, u32[]{:S(2)}) collective-permute-start(f32[4,4,4,1024]{3,2,1,0:T(4,128)S(1)} %get-tuple-element.43), channel_id=1, source_target_pairs={{0,1},{1,2},{2,3},{3,4},{4,5},{5,6},{6,7},{8,9},{9,10},{10,11},{11... | collective-permute-start | bytes 786440 | tf_op jit(solution)/shard_map/ppermute | solution.py:38
  77.1 9.8 %collective-permute-start.5 = (f32[4,4,4,1024]{3,2,1,0:T(4,128)S(1)}, f32[4,4,4,1024]{3,2,1,0:T(4,128)S(1)}, u32[]{:S(2)}, u32[]{:S(2)}) collective-permute-start(f32[4,4,4,1024]{3,2,1,0:T(4,128)S(1)} %get-tuple-element.44), channel_id=1, source_target_pairs={{1,0},{2,1},{3,2},{4,3},{5,4},{6,5},{7,6},{9,8},{10,9},{11,10},{12... | collective-permute-start | bytes 786440 | tf_op jit(solution)/shard_map/ppermute | solution.py:39
  98.7 1.3 copy-start
where the time goes:
time: 130 us
  blocking collectives  47.4 us (36%)
  other arithmetic  29.3 us (23%)
  local copies, waits for them, and re-layouts  23.5 us (18%)
  starting transfers between devices  17.3 us (13%)
  waiting for transfers between devices  11.8 us (9%)
    all_gather x2, blocking collectives, all_blocks(): parts = lax.all_gather(parts, axes[k])  29.1 us
    all_to_all x1, blocking collectives, sent_and_summed(): lax.all_to_all(cut_along(array, dim, length), axis, 0, 0, tiled=True)  18.3 us
    ppermute x3, starting transfers between devices, with_halo(): before = lax.ppermute(last, axis, up)  13.5 us
    ppermute x3, waiting for transfers between devices, with_halo(): after = lax.ppermute(leading, axis, down)  8.99 us
    mul x3, other arithmetic, adjoint_step(): coefficients[2] * values  7.71 us
    slice x9, local copies, waits for them, and re-layouts, spread(): jnp.roll(middle, 1, -1)  6.88 us
    add x3, other arithmetic, forward_step(): values[..., 1:-1, :]  6.72 us
    slice x6, local copies, waits for them, and re-layouts, spread(): jnp.roll(middle, -1, -1) - middle  4.74 us
  transfers between devices with their start and end apart: 6, of which 3 were waited for; matrix products, arithmetic and copies ran while one was open for 7% of the time, Pallas kernels for 0%

commit v1 on v0

v1 whole, which is shorter than its diff:
```python
import jax
import jax.numpy as jnp
from jax import lax
from jax.experimental import pallas as pl
from jax.experimental.pallas import tpu as pltpu
from jax.sharding import Mesh
from jax.sharding import PartitionSpec as P

SWEEP = 4
MEM = ("mem_0", "mem_1", "mem_2")
CHIP = ("mem_0", "mem_1")
HALO = 2 * SWEEP
GROUP = 32
LANES = 128


def regroup(tiles, lane):
    result = []
    for j in range(4):
        value = None
        for l in range(4):
            moved = tiles[l] if l == j else pltpu.roll(tiles[l], ((l - j) * GROUP) % LANES, 1)
            value = moved if value is None else jnp.where(lane < l * GROUP, value, moved)
        result.append(value)
    return result


def kernel(flags, perturb, k_north, k_east, scale, low, high, mine, other,
           keep, send, field, member, north, east, step, inverse, total):
    levels, rows, width = k_north.shape
    span = rows + 2 * HALO
    tiles = width // LANES
    core = flags[0]
    is_top = flags[1]

    row = lax.broadcasted_iota(jnp.int32, (rows, LANES), 0)
    edge = (row == rows - 1) & (is_top == 1)
    for t in range(tiles):
        cols = slice(t * LANES, (t + 1) * LANES)
        for l in range(levels):
            for m in range(4):
                at = (m // 2) * 8 + 2 * l + m % 2
                member[t, pl.ds(at, HALO, stride=16), :] = low[4 * m + l, :, cols]
                member[t, pl.ds(HALO * 16 + at, rows, stride=16), :] = perturb[
                    m, l, :, cols
                ].astype(jnp.float32)
                member[t, pl.ds((HALO + rows) * 16 + at, HALO, stride=16), :] = high[
                    4 * m + l, :, cols
                ]
            masked = jnp.where(edge, 0.0, k_north[l, :, cols])
            middles = ((north, masked), (east, k_east[l, :, cols]), (step, scale[l, :, cols]))
            for a, (ref, middle) in enumerate(middles):
                for twin in range(2):
                    at = 2 * l + twin
                    ref[t, pl.ds(at, HALO, stride=8), :] = low[16 + 4 * a + l, :, cols]
                    ref[t, pl.ds(HALO * 8 + at, rows, stride=8), :] = middle
                    ref[t, pl.ds((HALO + rows) * 8 + at, HALO, stride=8), :] = high[
                        16 + 4 * a + l, :, cols
                    ]

    lane = lax.broadcasted_iota(jnp.int32, (span, LANES), 1)
    for t in range(tiles):
        blocks = []
        for j in range(4):
            chip, owner = 2 * t + j // 2, j % 2
            blocks.append(jnp.where(core == owner, mine[chip], other[chip]))
        for l, value in enumerate(regroup(blocks, lane)):
            for twin in range(2):
                inverse[t, pl.ds(2 * l + twin, span, stride=8), :] = value

    def at8(j):
        return pl.ds(pl.multiple_of(j * 8, 8), 8)

    def at16(j, pair):
        return pl.ds(pl.multiple_of(j * 16 + 8 * pair, 8), 8)

    def start(j, _):
        for t in range(tiles):
            s = step[t, at8(j), :]
            sg = s * inverse[t, at8(j), :]
            for pair in range(2):
                field[t, at16(j, pair), :] = member[t, at16(j, pair), :] * sg
            inverse[t, at8(j), :] = 1.0 / jnp.where(s == 0.0, 1.0, s)
        return 0

    lax.fori_loop(0, span, start, 0)

    lane = lax.broadcasted_iota(jnp.int32, (8, LANES), 1)

    def shifted(values, amount):
        moved = [pltpu.roll(v, amount % LANES, 1) for v in values]
        edge = lane == (LANES - 1 if amount < 0 else 0)
        return [jnp.where(edge, moved[(t - amount) % tiles], moved[t]) for t in range(tiles)]

    def sweep(first, last, finish):
        for pair in range(2):
            def load(j):
                return [field[t, at16(j, pair), :] for t in range(tiles)]

            def one(j, carry):
                here, south = carry
                above = load(j + 1)
                flux = [north[t, at8(j), :] * (above[t] - here[t]) for t in range(tiles)]
                ahead = shifted(here, -1)
                side = [east[t, at8(j), :] * (ahead[t] - here[t]) for t in range(tiles)]
                behind = shifted(side, 1)
                for t in range(tiles):
                    change = (flux[t] - south[t]) + (side[t] - behind[t])
                    value = here[t] + step[t, at8(j), :] * change
                    if finish:
                        value = value * inverse[t, at8(j), :]
                    field[t, at16(j, pair), :] = value
                return above, flux

            here, before = load(first), load(first - 1)
            south = [north[t, at8(first - 1), :] * (here[t] - before[t]) for t in range(tiles)]
            lax.fori_loop(first, last, one, (here, south))

    for n in range(2 * SWEEP):
        sweep(n + 1, span - n - 1, n == SWEEP - 1)

    def gather(j, _):
        for t in range(tiles):
            value = None
            for pair in range(2):
                term = member[t, at16(j + HALO, pair), :] * field[t, at16(j + HALO, pair), :]
                value = term if value is None else value + term
            total[t, at8(j), :] = value
        return 0

    lax.fori_loop(0, rows, gather, 0)

    lane = lax.broadcasted_iota(jnp.int32, (rows, LANES), 1)
    for t in range(tiles):
        sums = [
            total[t, pl.ds(2 * l, rows, stride=8), :] + total[t, pl.ds(2 * l + 1, rows, stride=8), :]
            for l in range(levels)
        ]
        blocks = regroup(sums, lane)
        for k in range(2):
            a, b = blocks[2 * k], blocks[2 * k + 1]
            keep[2 * t + k] = jnp.where(core == 0, a, b)
            send[2 * t + k] = jnp.where(core == 0, b, a)


def shards(perturb, gradient, k_north, k_east, scale):
    members, levels, rows, width = perturb.shape
    span = rows + 2 * HALO
    size = lax.axis_size("lat")
    up = [(i, i + 1) for i in range(size - 1)]
    down = [(j, i) for i, j in up]
    swap = [(0, 1), (1, 0)]
    core = lax.axis_index("mem_2")
    is_top = (lax.axis_index("lat") == size - 1).astype(jnp.int32)
    flags = jnp.stack([core.astype(jnp.int32), is_top])

    packed = gradient.transpose(1, 0, 2).reshape(rows, levels * GROUP)
    below = lax.ppermute(packed[rows - HALO:], "lat", up)
    above = lax.ppermute(packed[:HALO], "lat", down)

    def edge(start):
        parts = [perturb[:, :, start:start + HALO].astype(jnp.float32).reshape(-1, HALO, width)]
        parts += [a[:, start:start + HALO] for a in (k_north, k_east, scale)]
        return jnp.concatenate(parts, axis=0)

    low = lax.ppermute(edge(rows - HALO), "lat", up)
    high = lax.ppermute(edge(0), "lat", down)

    chips = lax.axis_size(CHIP)
    block = jnp.concatenate([below, packed, above], axis=0)
    mine = lax.all_to_all(
        jnp.broadcast_to(block[None], (chips, span, LANES)), CHIP, 0, 0, tiled=True
    )
    other = lax.ppermute(mine, "mem_2", swap)

    vmem = pl.BlockSpec(memory_space=pltpu.VMEM)
    part = jax.ShapeDtypeStruct((chips, rows, LANES), jnp.float32)
    keep, send = pl.pallas_call(
        kernel,
        out_shape=(part, part),
        in_specs=[pl.BlockSpec(memory_space=pltpu.SMEM)] + [vmem] * 8,
        out_specs=(vmem, vmem),
        scratch_shapes=[
            pltpu.VMEM((width // LANES, span * 16, LANES), jnp.float32),
            pltpu.VMEM((width // LANES, span * 16, LANES), jnp.float32),
            pltpu.VMEM((width // LANES, span * 8, LANES), jnp.float32),
            pltpu.VMEM((width // LANES, span * 8, LANES), jnp.float32),
            pltpu.VMEM((width // LANES, span * 8, LANES), jnp.float32),
            pltpu.VMEM((width // LANES, span * 8, LANES), jnp.float32),
            pltpu.VMEM((width // LANES, rows * 8, LANES), jnp.float32),
        ],
        compiler_params=pltpu.CompilerParams(vmem_limit_bytes=40 * 2**20),
        name="diffuse",
    )(flags, perturb, k_north, k_east, scale, low, high, mine, other)

    merged = keep + lax.ppermute(send, "mem_2", swap)
    parts = lax.all_to_all(merged, CHIP, 0, 0, tiled=True)
    total = jnp.sum(parts, axis=0) / jnp.float32(members * lax.axis_size(MEM) - 1)
    return total.reshape(rows, levels, GROUP).transpose(1, 0, 2)


def solution(mesh):
    torus = Mesh(
        mesh.devices.reshape(4, 4, 2, mesh.shape["lat"]), ("mem_0", "mem_1", "mem_2", "lat")
    )
    in_specs = (
        P(MEM, None, "lat", None),
        P(None, "lat", MEM),
        P(None, "lat", None),
        P(None, "lat", None),
        P(None, "lat", None),
    )
    out_specs = P(None, "lat", MEM)
    return jax.shard_map(
        shards, mesh=torus, in_specs=in_specs, out_specs=out_specs, check_vma=False
    )
```

time: 130 us -> 167 us (1.28); the launches traced: 130 us -> 164 us
  Pallas kernels: 0 us -> 101 us
  other arithmetic: 29.3 us -> 2.33 us
  blocking collectives: 47.4 us -> 27 us
  local copies, waits for them, and re-layouts: 23.5 us -> 3.37 us
  waiting for transfers between devices: 11.8 us -> 14.8 us
  starting transfers between devices: 17.3 us -> 14.8 us
    pallas_call x0 -> x1, Pallas kernels: none -> 101 us  [shards(): pl.pallas_call(kernel, out_shape=(part, part), in_specs=[pl.BlockSpec(mem...]
    all_gather x2 -> x0, blocking collectives: 29.1 us -> none  [all_blocks(): parts = lax.all_gather(parts, axes[k])]
    slice x33 -> x8, local copies, waits for them, and re-layouts: 13 us -> 1.36 us  [the longest x1 1.12 us: edge(): perturb[:, :, start:start + HALO].astype(jnp.float32)]
    mul x4 -> x0, other arithmetic: 9.3 us -> none  [the longest x3 7.71 us: adjoint_step(): coefficients[2] * values]
    all_to_all x1 -> x2, blocking collectives: 18.3 us -> 27 us  [the longest x1 16.2 us: shards(): lax.all_to_all(jnp.broadcast_to(block[None], (chips, span, LANES)), CHIP,...]
    add x4 -> x1, other arithmetic: 8.54 us -> 0.04 us  [shards(): merged = keep + lax.ppermute(send, 'mem_2', swap)]
    transpose x3 -> x2, local copies, waits for them, and re-layouts: 4.05 us -> 0.68 us  [the longest x1 0.63 us: shards(): return total.reshape(rows, levels, GROUP).transpose(1, 0, 2)]
    slice x5 -> x0, other arithmetic: 3.01 us -> none  [the longest x1 1.87 us: with_halo(): last = lax.slice_in_dim(array, length - width, length, axis=dim)]
  transfers between devices with their start and end apart: 6 -> 6, of which waited for: 3 -> 3; matrix products, arithmetic and copies ran while one was open for 7% -> 1% of each run, Pallas kernels for 0% -> 0%
where the time goes in v1:
time: 167 us; the launch traced here: 164 us
  Pallas kernels  101 us (60%)
  blocking collectives  27 us (16%)
  starting transfers between devices  14.8 us (9%)
  waiting for transfers between devices  14.8 us (9%)
  local copies, waits for them, and re-layouts  3.37 us (2%)
  other arithmetic  2.33 us (1%)
    pallas_call x1, Pallas kernels, shards(): pl.pallas_call(kernel, out_shape=(part, part), in_specs=[pl.BlockSpec(mem...  101 us
    all_to_all x1, blocking collectives, shards(): lax.all_to_all(jnp.broadcast_to(block[None], (chips, span, LANES)), CHIP,...  16.2 us
    ppermute x1, waiting for transfers between devices, shards(): below = lax.ppermute(packed[rows - HALO:], 'lat', up)  12.3 us
    all_to_all x1, blocking collectives, shards(): parts = lax.all_to_all(merged, CHIP, 0, 0, tiled=True)  10.8 us
    ppermute x1, starting transfers between devices, shards(): low = lax.ppermute(edge(rows - HALO), 'lat', up)  6.1 us
  transfers between devices with their start and end apart: 6, of which 3 were waited for; matrix products, arithmetic and copies ran while one was open for 1% of the time, Pallas kernels for 0%

profile of v1, /device:TPU:1, one launch (start us, length us, event | category | flops | bytes accessed | tf_op | source)
XLA Modules:
  0.0 163.8 jit_solution(3019538815798793589)
XLA Ops:
  0.0 0.0 copy-start.3
  0.0 1.1 fusion
  1.1 0.0 copy-start.1
  1.1 0.0 copy-start.2
  1.2 0.1 bitcast_convert_fusion
  1.2 1.0 copy-done.1
  2.2 0.0 copy-done.3
  2.2 0.1 copy-done.2
  2.4 1.0 pad_maximum_fusion.1
  3.4 1.3 collective-permute-start.1
  4.7 0.1 bitcast_convert_fusion.1
  4.8 0.0 copy-start.4
  4.8 1.0 pad_maximum_fusion
  5.8 0.0 copy-start
  5.8 6.1 %collective-permute-start = (f32[28,8,1024]{2,1,0:T(8,128)}, f32[28,8,1024]{2,1,0:T(8,128)}, u32[]{:S(2)}, u32[]{:S(2)}) collective-permute-start(f32[28,8,1024]{2,1,0:T(8,128)} %pad_maximum_fusion), channel_id=1, source_target_pairs={{0,1},{1,2},{2,3},{3,4},{4,5},{5,6},{6,7},{8,9},{9,10},{10,11},{11... | collective-permute-start | bytes 2752520 | tf_op jit(solution)/shard_map/ppermute | solution.py:166
  11.9 0.0 copy-done.4
  11.9 0.1 slice.45
  12.0 2.6 %collective-permute-start.2 = (f32[8,128]{1,0:T(8,128)S(1)}, f32[8,128]{1,0:T(8,128)S(1)}, u32[]{:S(2)}, u32[]{:S(2)}) collective-permute-start(f32[8,128]{1,0:T(8,128)S(1)} %slice.45), channel_id=1, source_target_pairs={{0,1},{1,2},{2,3},{3,4},{4,5},{5,6},{6,7},{8,9},{9,10},{10,11},{11... | collective-permute-start | bytes 12296 | tf_op jit(solution)/shard_map/ppermute | solution.py:158
  14.6 0.1 slice.47
  14.7 1.3 collective-permute-start.3
  16.0 0.1 reshape.26
  16.1 12.3 %collective-permute-done.2 = f32[8,128]{1,0:T(8,128)S(1)} collective-permute-done((f32[8,128]{1,0:T(8,128)S(1)}, f32[8,128]{1,0:T(8,128)S(1)}, u32[]{:S(2)}, u32[]{:S(2)}) %collective-permute-start.2) | collective-permute-done | bytes 4128 | tf_op jit(solution)/shard_map/ppermute | solution.py:158
  28.5 0.0 collective-permute-done.3
  28.5 16.2 %all_to_all.10.mine = f32[16,48,128]{2,1,0:T(8,128)S(1)} all-to-all(f32[16,48,128]{2,1,0:T(8,128)S(1)} %broadcast_in_dim.2), channel_id=1, replica_groups=mesh['mem_0'=4,'mem_1'=4,'mem_2'=2,'lat'=8] {'mem_0','mem_1'}, dimensions={0} | all-to-all | bytes 786432 | tf_op jit(solution)/shard_map/all_to_all | solution.py:171
  44.8 3.1 %collective-permute-start.4 = (f32[16,48,128]{2,1,0:T(8,128)S(1)}, f32[16,48,128]{2,1,0:T(8,128)S(1)}, u32[]{:S(2)}, u32[]{:S(2)}) collective-permute-start(f32[16,48,128]{2,1,0:T(8,128)S(1)} %all_to_all.10.mine), channel_id=1, source_target_pairs={{0,8},{8,0},{1,9},{9,1},{2,10},{10,2},{3,11},{11,3},{4,12},{12,4},... | collective-permute-start | bytes 1179656 | tf_op jit(solution)/shard_map/ppermute | solution.py:174
  47.9 0.1 pad_add_fusion.flags
  47.9 1.3 collective-permute-done.4.other
  49.2 0.0 collective-permute-done.1.high
  49.2 0.0 collective-permute-done.low
  49.2 0.0 copy-done
  49.2 101.4 %diffuse.1 = (f32[16,32,128]{2,1,0:T(8,128)S(1)}, f32[16,32,128]{2,1,0:T(8,128)S(1)}) custom-call(s32[2]{0:T(128)S(1)} %pad_add_fusion.flags, bf16[4,4,32,1024]{3,2,1,0:T(8,128)(2,1)S(1)} %copy-done, f32[4,32,1024]{2,1,0:T(8,128)S(1)} %copy-done.2, f32[4,32,1024]{2,1,0:T(8,128)S(1)} %copy-done.3, f32[4,32,1024]{2,1,0:T(8,128)S(1)} %copy-done.1, ...), custom_call_target="tpu_custom_call" | custom-call | tf_op jit(solution)/shard_map/diffuse/pallas_call | solution.py:178
  150.6 0.5 collective-permute-start.5
  151.1 1.2 collective-permute-done.5
  152.3 10.8 %all_to_all.11 = f32[16,32,128]{2,1,0:T(8,128)S(1)} all-to-all(f32[16,32,128]{2,1,0:T(8,128)S(1)} %add.3), channel_id=1, replica_groups=mesh['mem_0'=4,'mem_1'=4,'mem_2'=2,'lat'=8] {'mem_0','mem_1'}, dimensions={0} | all-to-all | bytes 524288 | tf_op jit(solution)/shard_map/all_to_all | solution.py:197
  163.1 0.1 div.10
  163.2 0.6 copy.9
  (11 shorter events, 0.2 us)
Async XLA Ops:
  0.0 2.2 %copy-start.3 = (f32[4,32,1024]{2,1,0:T(8,128)S(1)}, f32[4,32,1024]{2,1,0:T(8,128)}, u32[]{:S(2)}) copy-start(f32[4,32,1024]{2,1,0:T(8,128)} %k_east.1) | copy-start | bytes 1572868
  1.1 1.0 copy-start.1
  1.1 1.2 copy-start.2
  3.4 45.8 %collective-permute-start.1 = (f32[28,8,1024]{2,1,0:T(8,128)}, f32[28,8,1024]{2,1,0:T(8,128)}, u32[]{:S(2)}, u32[]{:S(2)}) collective-permute-start(f32[28,8,1024]{2,1,0:T(8,128)} %pad_maximum_fusion.1), channel_id=1, source_target_pairs={{1,0},{2,1},{3,2},{4,3},{5,4},{6,5},{7,6},{9,8},{10,9},{11,10},{12... | collective-permute-start | bytes 2752520 | tf_op jit(solution)/shard_map/ppermute | solution.py:167
  4.8 7.2 %copy-start.4 = (f32[4,32,32]{2,1,0:T(8,128)S(1)}, f32[4,32,32]{2,1,0:T(8,128)}, u32[]{:S(2)}) copy-start(f32[4,32,32]{2,1,0:T(8,128)} %param.6) | copy-start | bytes 49156
  5.8 43.4 %copy-start = (bf16[4,4,32,1024]{3,2,1,0:T(8,128)(2,1)S(1)}, bf16[4,4,32,1024]{3,2,1,0:T(8,128)(2,1)}, u32[]{:S(2)}) copy-start(bf16[4,4,32,1024]{3,2,1,0:T(8,128)(2,1)} %perturb.1) | copy-start | bytes 3145732
  5.8 43.4 %collective-permute-start = (f32[28,8,1024]{2,1,0:T(8,128)}, f32[28,8,1024]{2,1,0:T(8,128)}, u32[]{:S(2)}, u32[]{:S(2)}) collective-permute-start(f32[28,8,1024]{2,1,0:T(8,128)} %pad_maximum_fusion), channel_id=1, source_target_pairs={{0,1},{1,2},{2,3},{3,4},{4,5},{5,6},{6,7},{8,9},{9,10},{10,11},{11... | collective-permute-start | bytes 2752520 | tf_op jit(solution)/shard_map/ppermute | solution.py:166
  12.0 16.4 %collective-permute-start.2 = (f32[8,128]{1,0:T(8,128)S(1)}, f32[8,128]{1,0:T(8,128)S(1)}, u32[]{:S(2)}, u32[]{:S(2)}) collective-permute-start(f32[8,128]{1,0:T(8,128)S(1)} %slice.45), channel_id=1, source_target_pairs={{0,1},{1,2},{2,3},{3,4},{4,5},{5,6},{6,7},{8,9},{9,10},{10,11},{11... | collective-permute-start | bytes 12296 | tf_op jit(solution)/shard_map/ppermute | solution.py:158
  14.7 13.8 %collective-permute-start.3 = (f32[8,128]{1,0:T(8,128)S(1)}, f32[8,128]{1,0:T(8,128)S(1)}, u32[]{:S(2)}, u32[]{:S(2)}) collective-permute-start(f32[8,128]{1,0:T(8,128)S(1)} %slice.47), channel_id=1, source_target_pairs={{1,0},{2,1},{3,2},{4,3},{5,4},{6,5},{7,6},{9,8},{10,9},{11,10},{12... | collective-permute-start | bytes 12296 | tf_op jit(solution)/shard_map/ppermute | solution.py:159
  44.8 4.5 %collective-permute-start.4 = (f32[16,48,128]{2,1,0:T(8,128)S(1)}, f32[16,48,128]{2,1,0:T(8,128)S(1)}, u32[]{:S(2)}, u32[]{:S(2)}) collective-permute-start(f32[16,48,128]{2,1,0:T(8,128)S(1)} %all_to_all.10.mine), channel_id=1, source_target_pairs={{0,8},{8,0},{1,9},{9,1},{2,10},{10,2},{3,11},{11,3},{4,12},{12,4},... | collective-permute-start | bytes 1179656 | tf_op jit(solution)/shard_map/ppermute | solution.py:174
  150.6 1.6 collective-permute-start.5

commit v2 on v0

v2 whole, which is shorter than its diff:
```python
import jax
import jax.numpy as jnp
from jax import lax
from jax.experimental import pallas as pl
from jax.experimental.pallas import tpu as pltpu
from jax.sharding import Mesh
from jax.sharding import PartitionSpec as P

SWEEP = 4
MEM = ("mem_0", "mem_1", "mem_2")
CHIP = ("mem_0", "mem_1")
HALO = 2 * SWEEP
GROUP = 32
LANES = 128
UNROLL = 4
F32 = jnp.float32
BF16 = jnp.bfloat16


def splitting(length, period):
    source = lax.broadcasted_iota(jnp.int32, (length, length), 0)
    target = lax.broadcasted_iota(jnp.int32, (length, length), 1)
    return one_hot(source, target, period)


def one_hot(source, target, period):
    inner = source & (period - 1)
    moved = (source - inner) + (inner & 1) * (period // 2) + (inner >> 1)
    return (moved == target).astype(F32).astype(BF16)


def exact_dot(values, matrix):
    high = values.astype(BF16)
    rest = values - high.astype(F32)
    mid = rest.astype(BF16)
    low = (rest - mid.astype(F32)).astype(BF16)

    def dot(part):
        return jnp.dot(part, matrix, preferred_element_type=F32)

    return (dot(high) + dot(mid)) + dot(low)


def exchange(values, lane):
    values = list(values)
    width = LANES // 8
    for d in (1, 2, 4):
        is_set = (lane & (width * d)) != 0
        for i in range(8):
            if i & d:
                continue
            a, b = values[i], values[i + d]
            values[i] = jnp.where(is_set, pltpu.roll(b, width * d, 1), a)
            values[i + d] = jnp.where(is_set, b, pltpu.roll(a, LANES - width * d, 1))
    return values


def at8(j):
    return pl.ds(pl.multiple_of(j * 8, 8), 8)


def at16(j, pair):
    return pl.ds(pl.multiple_of(j * 16 + 8 * pair, 8), 8)


def neighbours(values, lane):
    even, odd = values[:4], values[4:]
    east = [pltpu.roll(v, LANES - 1, 1) for v in even]
    west = [pltpu.roll(v, 1, 1) for v in odd]
    east = [jnp.where(lane == LANES - 1, east[(t + 1) % 4], east[t]) for t in range(4)]
    west = [jnp.where(lane == 0, west[(t - 1) % 4], west[t]) for t in range(4)]
    return odd + east, west + even


def pack_kernel(gradient, packed):
    joined = jnp.concatenate([gradient[l] for l in range(gradient.shape[0])], axis=1)
    packed[...] = exact_dot(joined, splitting(LANES, GROUP))


def edge_kernel(perturb, k_north, k_east, scale, out):
    for m in range(4):
        for l in range(4):
            out[4 * m + l] = perturb[m, l].astype(F32)
    for a, ref in enumerate((k_north, k_east, scale)):
        for l in range(4):
            out[16 + 4 * a + l] = ref[l]


def finish_kernel(count, parts, out):
    total = parts[0]
    for k in range(1, parts.shape[0]):
        total = total + parts[k]
    total = total / F32(count)
    source = lax.broadcasted_iota(jnp.int32, (LANES, LANES), 1)
    target = lax.broadcasted_iota(jnp.int32, (LANES, LANES), 0)
    total = exact_dot(total, one_hot(source, target, GROUP))
    for l in range(out.shape[0]):
        out[l] = total[:, l * GROUP:(l + 1) * GROUP]


def coefficients(rows, refs, lane):
    north, east, step, to_north, to_south, to_east, to_west, centre, inverse = refs

    def one(j):
        s = [step[t, at8(j), :] for t in range(8)]
        e = [east[t, at8(j), :] for t in range(8)]
        _, w = neighbours(e, lane)
        for t in range(8):
            up = s[t] * north[t, at8(j), :]
            down = s[t] * north[t, at8(j - 1), :]
            right = s[t] * e[t]
            left = s[t] * w[t]
            to_north[t, at8(j), :] = up
            to_south[t, at8(j), :] = down
            to_east[t, at8(j), :] = right
            to_west[t, at8(j), :] = left
            centre[t, at8(j), :] = 1.0 - ((up + down) + (right + left))
            inverse[t, at8(j), :] = 1.0 / jnp.where(s[t] == 0.0, 1.0, s[t])

    first, last = rows
    lax.fori_loop(first, last, lambda j, _: (one(j), 0)[1], 0)


def prepare_kernel(flags, perturb, k_north, k_east, scale, member, *refs):
    levels, rows, width = k_north.shape
    north, east, step = refs[:3]
    matrix = splitting(256, 256)
    row = lax.broadcasted_iota(jnp.int32, (rows, 256), 0)
    edge = (row == rows - 1) & (flags[1] == 1)
    for u in range(width // 256):
        cols = slice(u * 256, (u + 1) * 256)
        for m in range(4):
            values = jnp.dot(
                perturb[m, :, :, cols].reshape(levels * rows, 256), matrix,
                preferred_element_type=F32,
            )
            for l in range(levels):
                at = HALO * 16 + (m // 2) * 8 + 2 * l + m % 2
                for odd in range(2):
                    member[u + 4 * odd, pl.ds(at, rows, stride=16), :] = values[
                        l * rows:(l + 1) * rows, odd * LANES:(odd + 1) * LANES
                    ]
        for ref, source in ((north, k_north), (east, k_east), (step, scale)):
            parts = [source[l, :, cols] for l in range(levels)]
            if ref is north:
                parts = [jnp.where(edge, 0.0, part) for part in parts]
            values = exact_dot(jnp.concatenate(parts, axis=0), matrix)
            for l in range(levels):
                for odd in range(2):
                    value = values[l * rows:(l + 1) * rows, odd * LANES:(odd + 1) * LANES]
                    for twin in range(2):
                        at = HALO * 8 + 2 * l + twin
                        ref[u + 4 * odd, pl.ds(at, rows, stride=8), :] = value
    lane = lax.broadcasted_iota(jnp.int32, (8, LANES), 1)
    coefficients((HALO + 1, HALO + rows), refs, lane)


def sweep_kernel(flags, low, high, mine, other, *args):
    keep, send = args[10:12]
    member, *refs = args[12:22]
    scratch = args[22:]
    step, (to_north, to_south, to_east, to_west, centre, inverse) = refs[2], refs[3:]
    fields, guess, total = scratch[:2], scratch[2], scratch[3]
    rows, levels, span = keep.shape[1], 4, mine.shape[1]
    core = flags[0]
    matrix = splitting(256, 256)
    lane = lax.broadcasted_iota(jnp.int32, (8, LANES), 1)

    for u in range(low.shape[2] // 256):
        cols = slice(u * 256, (u + 1) * 256)
        for source, first in ((low, 0), (high, HALO + rows)):
            values = jnp.dot(
                source[:16, :, cols].reshape(16 * HALO, 256).astype(BF16), matrix,
                preferred_element_type=F32,
            )
            for m in range(4):
                for l in range(levels):
                    at = first * 16 + (m // 2) * 8 + 2 * l + m % 2
                    k = (m * levels + l) * HALO
                    for odd in range(2):
                        member[u + 4 * odd, pl.ds(at, HALO, stride=16), :] = values[
                            k:k + HALO, odd * LANES:(odd + 1) * LANES
                        ]
            values = exact_dot(source[16:, :, cols].reshape(12 * HALO, 256), matrix)
            for a in range(3):
                for l in range(levels):
                    k = (a * levels + l) * HALO
                    for odd in range(2):
                        for twin in range(2):
                            at = first * 8 + 2 * l + twin
                            refs[a][u + 4 * odd, pl.ds(at, HALO, stride=8), :] = values[
                                k:k + HALO, odd * LANES:(odd + 1) * LANES
                            ]
    for t in range(8):
        last = (t, at8(HALO - 1), slice(None))
        refs[0][last] = jnp.where(flags[2] == 1, 0.0, refs[0][last])
    coefficients((1, HALO + 1), refs, lane)
    coefficients((HALO + rows, span), refs, lane)

    wide = lax.broadcasted_iota(jnp.int32, (span, LANES), 1)
    for u in range(4):
        blocks = []
        for k in range(8):
            chip, owner = 4 * u + k // 2, k % 2
            blocks.append(jnp.where(core == owner, mine[chip], other[chip]))
        for k, value in enumerate(exchange(blocks, wide)):
            l, odd = k // 2, k % 2
            for twin in range(2):
                guess[u + 4 * odd, pl.ds(2 * l + twin, span, stride=8), :] = value

    def start(j, _):
        for t in range(8):
            scaled = step[t, at8(j), :] * guess[t, at8(j), :]
            for pair in range(2):
                fields[0][t, at16(j, pair), :] = member[t, at16(j, pair), :] * scaled
        return 0

    lax.fori_loop(0, span, start, 0)

    def advance(source, target, first, count, finish):
        def chunk(i, _):
            for k in range(UNROLL):
                j = first + i * UNROLL + k
                for pair in range(2):
                    here = [source[t, at16(j, pair), :] for t in range(8)]
                    right, left = neighbours(here, lane)
                    for t in range(8):
                        value = centre[t, at8(j), :] * here[t]
                        value += to_north[t, at8(j), :] * source[t, at16(j + 1, pair), :]
                        value += to_south[t, at8(j), :] * source[t, at16(j - 1, pair), :]
                        side = to_east[t, at8(j), :] * right[t] + to_west[t, at8(j), :] * left[t]
                        value += side
                        if finish:
                            value = value * inverse[t, at8(j), :]
                        target[t, at16(j, pair), :] = value
            return 0

        lax.fori_loop(0, -(-count // UNROLL), chunk, 0)

    for n in range(2 * SWEEP):
        advance(fields[n % 2], fields[1 - n % 2], n + 1, span - 2 * n - 2, n == SWEEP - 1)
    result = fields[0]

    def gather(j, _):
        for t in range(8):
            value = None
            for pair in range(2):
                term = member[t, at16(j + HALO, pair), :] * result[t, at16(j + HALO, pair), :]
                value = term if value is None else value + term
            total[t, at8(j), :] = value
        return 0

    lax.fori_loop(0, rows, gather, 0)

    wide = lax.broadcasted_iota(jnp.int32, (rows, LANES), 1)
    for u in range(4):
        sums = []
        for k in range(8):
            l, t = k // 2, u + 4 * (k % 2)
            sums.append(
                total[t, pl.ds(2 * l, rows, stride=8), :]
                + total[t, pl.ds(2 * l + 1, rows, stride=8), :]
            )
        blocks = exchange(sums, wide)
        for k in range(4):
            a, b = blocks[2 * k], blocks[2 * k + 1]
            keep[4 * u + k] = jnp.where(core == 0, a, b)
            send[4 * u + k] = jnp.where(core == 0, b, a)


def shards(perturb, gradient, k_north, k_east, scale):
    members, levels, rows, width = perturb.shape
    span = rows + 2 * HALO
    size = lax.axis_size("lat")
    up = [(i, (i + 1) % size) for i in range(size)]
    down = [(j, i) for i, j in up]
    swap = [(0, 1), (1, 0)]
    core = lax.axis_index("mem_2")
    place = lax.axis_index("lat")
    flags = jnp.stack([core, place == size - 1, place == 0]).astype(jnp.int32)
    vmem = pl.BlockSpec(memory_space=pltpu.VMEM)
    smem = pl.BlockSpec(memory_space=pltpu.SMEM)

    packed = pl.pallas_call(
        pack_kernel,
        out_shape=jax.ShapeDtypeStruct((rows, LANES), F32),
        in_specs=[vmem], out_specs=vmem, name="pack",
    )(gradient)
    below = lax.ppermute(packed[rows - HALO:], "lat", up)
    above = lax.ppermute(packed[:HALO], "lat", down)

    def edge(block):
        short = pl.BlockSpec((levels, HALO, width), lambda i: (0, block, 0))
        return pl.pallas_call(
            edge_kernel,
            out_shape=jax.ShapeDtypeStruct((7 * levels, HALO, width), F32),
            grid=(1,),
            in_specs=[pl.BlockSpec((4, levels, HALO, width), lambda i: (0, 0, block, 0))] + [short] * 3,
            out_specs=pl.BlockSpec((7 * levels, HALO, width), lambda i: (0, 0, 0)),
            compiler_params=pltpu.CompilerParams(vmem_limit_bytes=8 * 2**20),
            cost_estimate=pl.CostEstimate(flops=0, bytes_accessed=2 * 2**20, transcendentals=0),
            name="edges",
        )(perturb, k_north, k_east, scale)

    top, bottom = edge(rows // HALO - 1), edge(0)
    low = lax.ppermute(top, "lat", up)
    high = lax.ppermute(bottom, "lat", down)

    chips = lax.axis_size(CHIP)
    block = jnp.concatenate([below, packed, above], axis=0)
    spread = jnp.broadcast_to(block[None], (chips, span, LANES))
    mine = lax.all_to_all(spread, CHIP, 0, 0, tiled=True)
    other = lax.ppermute(mine, "mem_2", swap)

    padded = span + UNROLL
    tall = pltpu.VMEM((8, padded * 16, LANES), F32)
    short = pltpu.VMEM((8, padded * 8, LANES), F32)
    prepare = pl.pallas_call(
        prepare_kernel,
        out_shape=[tall] + [short] * 9,
        in_specs=[smem] + [vmem] * 4,
        out_specs=[vmem] * 10,
        compiler_params=pltpu.CompilerParams(vmem_limit_bytes=8 * 2**20),
        cost_estimate=pl.CostEstimate(flops=0, bytes_accessed=24 * 2**20, transcendentals=0),
        name="prepare",
    )
    prepared = prepare(flags, perturb, k_north, k_east, scale)

    part = jax.ShapeDtypeStruct((chips, rows, LANES), F32)
    keep, send = pl.pallas_call(
        sweep_kernel,
        out_shape=[part, part] + [tall] + [short] * 9,
        in_specs=[smem] + [vmem] * 14,
        out_specs=[vmem] * 12,
        input_output_aliases={5 + k: 2 + k for k in range(10)},
        scratch_shapes=[
            tall,
            tall,
            pltpu.VMEM((8, span * 8, LANES), F32),
            pltpu.VMEM((8, rows * 8, LANES), F32),
        ],
        compiler_params=pltpu.CompilerParams(vmem_limit_bytes=18 * 2**20),
        name="sweeps",
    )(flags, low, high, mine, other, *prepared)[:2]

    merged = keep + lax.ppermute(send, "mem_2", swap)
    parts = lax.all_to_all(merged, CHIP, 0, 0, tiled=True)
    count = members * lax.axis_size(MEM) - 1
    return pl.pallas_call(
        lambda p, o: finish_kernel(count, p, o),
        out_shape=jax.ShapeDtypeStruct((levels, rows, GROUP), F32),
        in_specs=[vmem], out_specs=vmem, name="finish",
    )(parts)


def solution(mesh):
    torus = Mesh(
        mesh.devices.reshape(4, 4, 2, mesh.shape["lat"]), ("mem_0", "mem_1", "mem_2", "lat")
    )
    in_specs = (
        P(MEM, None, "lat", None),
        P(None, "lat", MEM),
        P(None, "lat", None),
        P(None, "lat", None),
        P(None, "lat", None),
    )
    out_specs = P(None, "lat", MEM)

    return jax.shard_map(
        shards, mesh=torus, in_specs=in_specs, out_specs=out_specs, check_vma=False
    )
```

time: 130 us -> 93.8 us (0.72)
  Pallas kernels: 0 us -> 30.1 us
  other arithmetic: 29.3 us -> 0.84 us
  blocking collectives: 47.4 us -> 25.7 us
  local copies, waits for them, and re-layouts: 23.5 us -> 5.1 us
  waiting for transfers between devices: 11.8 us -> 19.1 us
  starting transfers between devices: 17.3 us -> 12.4 us
    pallas_call x0 -> x6, Pallas kernels: none -> 30.1 us  [the longest x1 19.8 us: shards(): pl.pallas_call(sweep_kernel, out_shape=[part, part] + [tall] + [short] *...]
    all_gather x2 -> x0, blocking collectives: 29.1 us -> none  [all_blocks(): parts = lax.all_gather(parts, axes[k])]
    slice x33 -> x1, local copies, waits for them, and re-layouts: 13 us -> 0.7 us  [shards(): below = lax.ppermute(packed[rows - HALO:], 'lat', up)]
    mul x4 -> x0, other arithmetic: 9.3 us -> none  [the longest x3 7.71 us: adjoint_step(): coefficients[2] * values]
    add x4 -> x1, other arithmetic: 8.54 us -> 0.04 us  [shards(): merged = keep + lax.ppermute(send, 'mem_2', swap)]
    all_to_all x1 -> x2, blocking collectives: 18.3 us -> 25.7 us  [the longest x1 14.5 us: shards(): mine = lax.all_to_all(spread, CHIP, 0, 0, tiled=True)]
    ppermute x6, waiting for transfers between devices: 11.8 us -> 19.1 us  [the longest x1 17.5 us: shards(): below = lax.ppermute(packed[rows - HALO:], 'lat', up)]
    ppermute x6, starting transfers between devices: 17.3 us -> 12.4 us  [the longest x1 6.47 us: shards(): high = lax.ppermute(bottom, 'lat', down)]
  transfers between devices with their start and end apart: 6 -> 6, of which waited for: 3 -> 2; matrix products, arithmetic and copies ran while one was open for 7% -> 2% of each run, Pallas kernels for 0% -> 8%
where the time goes in v2:
time: 93.8 us; the launch traced here: 93.3 us
  Pallas kernels  30.1 us (32%)
  blocking collectives  25.7 us (27%)
  waiting for transfers between devices  19.1 us (20%)
  starting transfers between devices  12.4 us (13%)
  local copies, waits for them, and re-layouts  5.1 us (5%)
    pallas_call x1, Pallas kernels, shards(): pl.pallas_call(sweep_kernel, out_shape=[part, part] + [tall] + [short] *...  19.8 us
    ppermute x1, waiting for transfers between devices, shards(): below = lax.ppermute(packed[rows - HALO:], 'lat', up)  17.5 us
    all_to_all x1, blocking collectives, shards(): mine = lax.all_to_all(spread, CHIP, 0, 0, tiled=True)  14.5 us
    all_to_all x1, blocking collectives, shards(): parts = lax.all_to_all(merged, CHIP, 0, 0, tiled=True)  11.1 us
    ppermute x1, starting transfers between devices, shards(): high = lax.ppermute(bottom, 'lat', down)  6.47 us
    pallas_call x1, Pallas kernels, shards(): prepared = prepare(flags, perturb, k_north, k_east, scale)  4.88 us
    unnamed x16, local copies, waits for them, and re-layouts  4.36 us
    ppermute x1, starting transfers between devices, shards(): other = lax.ppermute(mine, 'mem_2', swap)  3.2 us
  transfers between devices with their start and end apart: 6, of which 2 were waited for; matrix products, arithmetic and copies ran while one was open for 2% of the time, Pallas kernels for 8%

profile of v2, /device:TPU:1, one launch (start us, length us, event | category | flops | bytes accessed | tf_op | source)
XLA Modules:
  0.0 93.3 jit_solution(5406898473390174683)
XLA Ops:
  0.0 0.0 copy-start
  0.0 1.2 %copy-done = bf16[4,4,32,1024]{3,2,1,0:T(8,128)(2,1)S(1)} copy-done((bf16[4,4,32,1024]{3,2,1,0:T(8,128)(2,1)S(1)}, bf16[4,4,32,1024]{3,2,1,0:T(8,128)(2,1)}, u32[]{:S(2)}) %copy-start) | copy-done | bytes 1048600
  1.2 0.0 copy-start.2
  1.2 1.0 %copy-done.2 = f32[4,32,1024]{2,1,0:T(8,128)S(1)} copy-done((f32[4,32,1024]{2,1,0:T(8,128)S(1)}, f32[4,32,1024]{2,1,0:T(8,128)}, u32[]{:S(2)}) %copy-start.2) | copy-done | bytes 524312
  2.3 0.0 copy-start.4
  2.3 1.0 %copy-done.4 = f32[4,32,1024]{2,1,0:T(8,128)S(1)} copy-done((f32[4,32,1024]{2,1,0:T(8,128)S(1)}, f32[4,32,1024]{2,1,0:T(8,128)}, u32[]{:S(2)}) %copy-start.4) | copy-done | bytes 524312
  3.3 0.0 copy-start.6
  3.3 1.0 %copy-done.6 = f32[4,32,1024]{2,1,0:T(8,128)S(1)} copy-done((f32[4,32,1024]{2,1,0:T(8,128)S(1)}, f32[4,32,1024]{2,1,0:T(8,128)}, u32[]{:S(2)}) %copy-start.6) | copy-done | bytes 524312
  4.4 1.0 %edges.3 = f32[28,8,1024]{2,1,0:T(8,128)} custom-call(bf16[4,4,32,1024]{3,2,1,0:T(8,128)(2,1)S(1)} %copy-done, f32[4,32,1024]{2,1,0:T(8,128)S(1)} %copy-done.2, f32[4,32,1024]{2,1,0:T(8,128)S(1)} %copy-done.4, f32[4,32,1024]{2,1,0:T(8,128)S(1)} %copy-done.6), custom_call_target="tpu_custom_call" | custom-call | bytes 2097152 | tf_op jit(solution)/shard_map/edges/pallas_call | solution.py:294
  5.4 0.0 copy-start.1
  5.4 0.0 copy-start.3
  5.4 0.0 copy-start.5
  5.4 0.0 copy-start.7
  5.4 6.5 %collective-permute-start.1 = (f32[28,8,1024]{2,1,0:T(8,128)}, f32[28,8,1024]{2,1,0:T(8,128)}, u32[]{:S(2)}, u32[]{:S(2)}) collective-permute-start(f32[28,8,1024]{2,1,0:T(8,128)} %edges.3), channel_id=1, source_target_pairs={{1,0},{2,1},{3,2},{4,3},{5,4},{6,5},{7,6},{0,7},{9,8},{10,9},{11,1... | collective-permute-start | bytes 2752520 | tf_op jit(solution)/shard_map/ppermute | solution.py:307
  11.8 1.0 %edges.2 = f32[28,8,1024]{2,1,0:T(8,128)} custom-call(bf16[4,4,32,1024]{3,2,1,0:T(8,128)(2,1)S(1)} %copy-done, f32[4,32,1024]{2,1,0:T(8,128)S(1)} %copy-done.2, f32[4,32,1024]{2,1,0:T(8,128)S(1)} %copy-done.4, f32[4,32,1024]{2,1,0:T(8,128)S(1)} %copy-done.6), custom_call_target="tpu_custom_call" | custom-call | bytes 2097152 | tf_op jit(solution)/shard_map/edges/pallas_call | solution.py:294
  12.8 0.0 collective-permute-start
  12.8 1.7 %pack.1 = f32[32,128]{1,0:T(8,128)} custom-call(f32[4,32,32]{2,1,0:T(8,128)} %gradient.1), custom_call_target="tpu_custom_call" | custom-call | tf_op jit(solution)/shard_map/pack/pallas_call | solution.py:284
  14.5 0.7 fusion
  15.2 0.0 collective-permute-start.2
  15.2 2.7 %collective-permute-start.3 = (f32[8,128]{1,0:T(8,128)S(1)}, f32[8,128]{1,0:T(8,128)S(1)}, u32[]{:S(2)}, u32[]{:S(2)}) collective-permute-start(f32[8,128]{1,0:T(8,128)S(1)} %get-tuple-element.30), channel_id=1, source_target_pairs={{1,0},{2,1},{3,2},{4,3},{5,4},{6,5},{7,6},{0,7},{9,8},{10,9},{11,1... | collective-permute-start | bytes 12296 | tf_op jit(solution)/shard_map/ppermute | solution.py:290
  17.9 17.5 %collective-permute-done.2 = f32[8,128]{1,0:T(8,128)S(1)} collective-permute-done((f32[8,128]{1,0:T(8,128)S(1)}, f32[8,128]{1,0:T(8,128)S(1)}, u32[]{:S(2)}, u32[]{:S(2)}) %collective-permute-start.2) | collective-permute-done | bytes 4128 | tf_op jit(solution)/shard_map/ppermute | solution.py:289
  35.4 0.0 collective-permute-done.3
  35.4 0.7 pad_maximum_fusion
  36.2 14.5 %all_to_all.10.mine = f32[16,48,128]{2,1,0:T(8,128)S(1)} all-to-all(f32[16,48,128]{2,1,0:T(8,128)S(1)} %broadcast_in_dim.2), channel_id=1, replica_groups=mesh['mem_0'=4,'mem_1'=4,'mem_2'=2,'lat'=8] {'mem_0','mem_1'}, dimensions={0} | all-to-all | bytes 786432 | tf_op jit(solution)/shard_map/all_to_all | solution.py:312
  50.7 3.2 %collective-permute-start.4 = (f32[16,48,128]{2,1,0:T(8,128)S(1)}, f32[16,48,128]{2,1,0:T(8,128)S(1)}, u32[]{:S(2)}, u32[]{:S(2)}) collective-permute-start(f32[16,48,128]{2,1,0:T(8,128)S(1)} %all_to_all.10.mine), channel_id=1, source_target_pairs={{0,8},{8,0},{1,9},{9,1},{2,10},{10,2},{3,11},{11,3},{4,12},{12,4},... | collective-permute-start | bytes 1179656 | tf_op jit(solution)/shard_map/ppermute | solution.py:313
  53.9 0.1 pad_add_fusion.flags
  54.0 0.0 copy-done.1
  54.0 0.0 copy-done.3
  54.0 0.0 copy-done.5
  54.0 0.0 copy-done.7
  54.0 4.9 %prepare.1 = (f32[8,832,128]{2,1,0:T(8,128)S(1)}, f32[8,416,128]{2,1,0:T(8,128)S(1)}, f32[8,416,128]{2,1,0:T(8,128)S(1)}, f32[8,416,128]{2,1,0:T(8,128)S(1)}, f3...) custom-call(s32[3]{0:T(128)S(1)} %pad_add_fusion.flags, ...), custom_call_target="tpu_custom_call" | custom-call | bytes 25165824 | tf_op jit(solution)/shard_map/prepare/pallas_call | solution.py:327
  58.9 0.0 collective-permute-done.4.other
  58.9 0.0 collective-permute-done.1.high
  58.9 0.0 collective-permute-done.low
  58.9 19.8 %sweeps.1 = (f32[16,32,128]{2,1,0:T(8,128)S(1)}, f32[16,32,128]{2,1,0:T(8,128)S(1)}, f32[8,832,128]{2,1,0:T(8,128)S(1)}, f32[8,416,128]{2,1,0:T(8,128)S(1)}, f32...) custom-call(s32[3]{0:T(128)S(1)} %pad_add_fusion.flags, ...), custom_call_target="tpu_custom_call", output_to_operand_aliasing={{2}: (5, {}), {3}: (6, {}), {4}: (7, {}), {5}: (8, {}), {6}... | custom-call | tf_op jit(solution)/shard_map/sweeps/pallas_call | solution.py:330
  78.7 0.1 collective-permute-start.5
  78.8 1.5 %collective-permute-done.5 = f32[16,32,128]{2,1,0:T(8,128)S(1)} collective-permute-done((f32[16,32,128]{2,1,0:T(8,128)S(1)}, f32[16,32,128]{2,1,0:T(8,128)S(1)}, u32[]{:S(2)}, u32[]{:S(2)}) %collective-permute-start.5) | collective-permute-done | bytes 262176 | tf_op jit(solution)/shard_map/ppermute | solution.py:346
  80.3 11.1 %all_to_all.11.p = f32[16,32,128]{2,1,0:T(8,128)} all-to-all(f32[16,32,128]{2,1,0:T(8,128)S(1)} %add.3), channel_id=1, replica_groups=mesh['mem_0'=4,'mem_1'=4,'mem_2'=2,'lat'=8] {'mem_0','mem_1'}, dimensions={0} | all-to-all | bytes 524288 | tf_op jit(solution)/shard_map/all_to_all | solution.py:347
  91.5 1.8 %finish.1 = f32[4,32,32]{2,1,0:T(8,128)} custom-call(f32[16,32,128]{2,1,0:T(8,128)} %all_to_all.11.p), custom_call_target="tpu_custom_call" | custom-call | tf_op jit(solution)/shard_map/finish/pallas_call | solution.py:349
  (2 shorter events, 0.1 us)
Async XLA Ops:
  0.0 1.2 %copy-start = (bf16[4,4,32,1024]{3,2,1,0:T(8,128)(2,1)S(1)}, bf16[4,4,32,1024]{3,2,1,0:T(8,128)(2,1)}, u32[]{:S(2)}) copy-start(bf16[4,4,32,1024]{3,2,1,0:T(8,128)(2,1)} %perturb.5) | copy-start | bytes 3145732
  1.2 1.0 %copy-start.2 = (f32[4,32,1024]{2,1,0:T(8,128)S(1)}, f32[4,32,1024]{2,1,0:T(8,128)}, u32[]{:S(2)}) copy-start(f32[4,32,1024]{2,1,0:T(8,128)} %k_north.5) | copy-start | bytes 1572868
  2.3 1.0 %copy-start.4 = (f32[4,32,1024]{2,1,0:T(8,128)S(1)}, f32[4,32,1024]{2,1,0:T(8,128)}, u32[]{:S(2)}) copy-start(f32[4,32,1024]{2,1,0:T(8,128)} %k_east.5) | copy-start | bytes 1572868
  3.3 1.0 %copy-start.6 = (f32[4,32,1024]{2,1,0:T(8,128)S(1)}, f32[4,32,1024]{2,1,0:T(8,128)}, u32[]{:S(2)}) copy-start(f32[4,32,1024]{2,1,0:T(8,128)} %scale.5) | copy-start | bytes 1572868
  5.4 48.6 %copy-start.1 = (bf16[4,4,32,1024]{3,2,1,0:T(8,128)(2,1)S(1)}, bf16[4,4,32,1024]{3,2,1,0:T(8,128)(2,1)}, u32[]{:S(2)}) copy-start(bf16[4,4,32,1024]{3,2,1,0:T(8,128)(2,1)} %perturb.5) | copy-start | bytes 3145732
  5.4 48.6 %copy-start.3 = (f32[4,32,1024]{2,1,0:T(8,128)S(1)}, f32[4,32,1024]{2,1,0:T(8,128)}, u32[]{:S(2)}) copy-start(f32[4,32,1024]{2,1,0:T(8,128)} %k_north.5) | copy-start | bytes 1572868
  5.4 48.6 %copy-start.5 = (f32[4,32,1024]{2,1,0:T(8,128)S(1)}, f32[4,32,1024]{2,1,0:T(8,128)}, u32[]{:S(2)}) copy-start(f32[4,32,1024]{2,1,0:T(8,128)} %k_east.5) | copy-start | bytes 1572868
  5.4 48.6 %copy-start.7 = (f32[4,32,1024]{2,1,0:T(8,128)S(1)}, f32[4,32,1024]{2,1,0:T(8,128)}, u32[]{:S(2)}) copy-start(f32[4,32,1024]{2,1,0:T(8,128)} %scale.5) | copy-start | bytes 1572868
  5.4 53.5 %collective-permute-start.1 = (f32[28,8,1024]{2,1,0:T(8,128)}, f32[28,8,1024]{2,1,0:T(8,128)}, u32[]{:S(2)}, u32[]{:S(2)}) collective-permute-start(f32[28,8,1024]{2,1,0:T(8,128)} %edges.3), channel_id=1, source_target_pairs={{1,0},{2,1},{3,2},{4,3},{5,4},{6,5},{7,6},{0,7},{9,8},{10,9},{11,1... | collective-permute-start | bytes 2752520 | tf_op jit(solution)/shard_map/ppermute | solution.py:307
  12.8 46.1 %collective-permute-start = (f32[28,8,1024]{2,1,0:T(8,128)}, f32[28,8,1024]{2,1,0:T(8,128)}, u32[]{:S(2)}, u32[]{:S(2)}) collective-permute-start(f32[28,8,1024]{2,1,0:T(8,128)} %edges.2), channel_id=1, source_target_pairs={{0,1},{1,2},{2,3},{3,4},{4,5},{5,6},{6,7},{7,0},{8,9},{9,10},{10,1... | collective-permute-start | bytes 2752520 | tf_op jit(solution)/shard_map/ppermute | solution.py:306
  15.2 20.2 %collective-permute-start.2 = (f32[8,128]{1,0:T(8,128)S(1)}, f32[8,128]{1,0:T(8,128)S(1)}, u32[]{:S(2)}, u32[]{:S(2)}) collective-permute-start(f32[8,128]{1,0:T(8,128)S(1)} %get-tuple-element.29), channel_id=1, source_target_pairs={{0,1},{1,2},{2,3},{3,4},{4,5},{5,6},{6,7},{7,0},{8,9},{9,10},{10,1... | collective-permute-start | bytes 12296 | tf_op jit(solution)/shard_map/ppermute | solution.py:289
  15.2 20.2 %collective-permute-start.3 = (f32[8,128]{1,0:T(8,128)S(1)}, f32[8,128]{1,0:T(8,128)S(1)}, u32[]{:S(2)}, u32[]{:S(2)}) collective-permute-start(f32[8,128]{1,0:T(8,128)S(1)} %get-tuple-element.30), channel_id=1, source_target_pairs={{1,0},{2,1},{3,2},{4,3},{5,4},{6,5},{7,6},{0,7},{9,8},{10,9},{11,1... | collective-permute-start | bytes 12296 | tf_op jit(solution)/shard_map/ppermute | solution.py:290
  50.7 8.2 %collective-permute-start.4 = (f32[16,48,128]{2,1,0:T(8,128)S(1)}, f32[16,48,128]{2,1,0:T(8,128)S(1)}, u32[]{:S(2)}, u32[]{:S(2)}) collective-permute-start(f32[16,48,128]{2,1,0:T(8,128)S(1)} %all_to_all.10.mine), channel_id=1, source_target_pairs={{0,8},{8,0},{1,9},{9,1},{2,10},{10,2},{3,11},{11,3},{4,12},{12,4},... | collective-permute-start | bytes 1179656 | tf_op jit(solution)/shard_map/ppermute | solution.py:313
  78.7 1.6 %collective-permute-start.5 = (f32[16,32,128]{2,1,0:T(8,128)S(1)}, f32[16,32,128]{2,1,0:T(8,128)S(1)}, u32[]{:S(2)}, u32[]{:S(2)}) collective-permute-start(f32[16,32,128]{2,1,0:T(8,128)S(1)} %get-tuple-element.28), channel_id=1, source_target_pairs={{0,8},{8,0},{1,9},{9,1},{2,10},{10,2},{3,11},{11,3},{4,12},{12,4},... | collective-permute-start | bytes 786440 | tf_op jit(solution)/shard_map/ppermute | solution.py:346

commit v3 on v2

--- a/solution.py
+++ b/solution.py
@@ -13,6 +13,7 @@
 GROUP = 32
 LANES = 128
 UNROLL = 4
+CLOSED = 66_150_400
 F32 = jnp.float32
 BF16 = jnp.bfloat16
 
@@ -72,18 +73,32 @@
     return odd + east, west + even
 
 
-def pack_kernel(gradient, packed):
+def edge_kernel(gradient, perturb, k_north, k_east, scale,
+                packed, first, last, top, bottom, narrow, sems):
+    rows = perturb.shape[2]
+    copies = []
+    for side, (out, start) in enumerate(((top, rows - HALO), (bottom, 0))):
+        at = pl.ds(start, HALO)
+        copies.append(pltpu.make_async_copy(
+            perturb.at[:, :, at, :], narrow.at[side], sems.at[side, 0]
+        ))
+        for a, ref in enumerate((k_north, k_east, scale)):
+            copies.append(pltpu.make_async_copy(
+                ref.at[:, at, :], out.at[pl.ds(16 + 4 * a, 4)], sems.at[side, 1 + a]
+            ))
+    for copy in copies:
+        copy.start()
     joined = jnp.concatenate([gradient[l] for l in range(gradient.shape[0])], axis=1)
-    packed[...] = exact_dot(joined, splitting(LANES, GROUP))
-
-
-def edge_kernel(perturb, k_north, k_east, scale, out):
-    for m in range(4):
-        for l in range(4):
-            out[4 * m + l] = perturb[m, l].astype(F32)
-    for a, ref in enumerate((k_north, k_east, scale)):
-        for l in range(4):
-            out[16 + 4 * a + l] = ref[l]
+    value = exact_dot(joined, splitting(LANES, GROUP))
+    packed[...] = value
+    first[...] = value[:HALO]
+    last[...] = value[-HALO:]
+    for copy in copies:
+        copy.wait()
+    for side, out in enumerate((top, bottom)):
+        for m in range(4):
+            for l in range(4):
+                out[4 * m + l] = narrow[side, m, l].astype(F32)
 
 
 def finish_kernel(count, parts, out):
@@ -117,16 +132,20 @@
             centre[t, at8(j), :] = 1.0 - ((up + down) + (right + left))
             inverse[t, at8(j), :] = 1.0 / jnp.where(s[t] == 0.0, 1.0, s[t])
 
-    first, last = rows
-    lax.fori_loop(first, last, lambda j, _: (one(j), 0)[1], 0)
-
-
-def prepare_kernel(flags, perturb, k_north, k_east, scale, member, *refs):
+    def chunk(i, _):
+        for k in range(UNROLL):
+            one(rows[0] + i * UNROLL + k)
+        return 0
+
+    lax.fori_loop(0, (rows[1] - rows[0]) // UNROLL, chunk, 0)
+
+
+def prepare_kernel(perturb, k_north, k_east, scale, member, *refs):
     levels, rows, width = k_north.shape
     north, east, step = refs[:3]
     matrix = splitting(256, 256)
     row = lax.broadcasted_iota(jnp.int32, (rows, 256), 0)
-    edge = (row == rows - 1) & (flags[1] == 1)
+    edge = (row == rows - 1) & (lax.axis_index("lat") == lax.axis_size("lat") - 1)
     for u in range(width // 256):
         cols = slice(u * 256, (u + 1) * 256)
         for m in range(4):
@@ -152,50 +171,22 @@
                         at = HALO * 8 + 2 * l + twin
                         ref[u + 4 * odd, pl.ds(at, rows, stride=8), :] = value
     lane = lax.broadcasted_iota(jnp.int32, (8, LANES), 1)
-    coefficients((HALO + 1, HALO + rows), refs, lane)
-
-
-def sweep_kernel(flags, low, high, mine, other, *args):
+    coefficients((HALO, HALO + rows), refs, lane)
+
+
+def sweep_kernel(low, high, mine, other, *args):
     keep, send = args[10:12]
     member, *refs = args[12:22]
     scratch = args[22:]
     step, (to_north, to_south, to_east, to_west, centre, inverse) = refs[2], refs[3:]
-    fields, guess, total = scratch[:2], scratch[2], scratch[3]
+    fields, guess, total, near, sems = scratch[:2], scratch[2], scratch[3], scratch[4], scratch[5]
     rows, levels, span = keep.shape[1], 4, mine.shape[1]
-    core = flags[0]
-    matrix = splitting(256, 256)
-    lane = lax.broadcasted_iota(jnp.int32, (8, LANES), 1)
-
-    for u in range(low.shape[2] // 256):
-        cols = slice(u * 256, (u + 1) * 256)
-        for source, first in ((low, 0), (high, HALO + rows)):
-            values = jnp.dot(
-                source[:16, :, cols].reshape(16 * HALO, 256).astype(BF16), matrix,
-                preferred_element_type=F32,
-            )
-            for m in range(4):
-                for l in range(levels):
-                    at = first * 16 + (m // 2) * 8 + 2 * l + m % 2
-                    k = (m * levels + l) * HALO
-                    for odd in range(2):
-                        member[u + 4 * odd, pl.ds(at, HALO, stride=16), :] = values[
-                            k:k + HALO, odd * LANES:(odd + 1) * LANES
-                        ]
-            values = exact_dot(source[16:, :, cols].reshape(12 * HALO, 256), matrix)
-            for a in range(3):
-                for l in range(levels):
-                    k = (a * levels + l) * HALO
-                    for odd in range(2):
-                        for twin in range(2):
-                            at = first * 8 + 2 * l + twin
-                            refs[a][u + 4 * odd, pl.ds(at, HALO, stride=8), :] = values[
-                                k:k + HALO, odd * LANES:(odd + 1) * LANES
-                            ]
-    for t in range(8):
-        last = (t, at8(HALO - 1), slice(None))
-        refs[0][last] = jnp.where(flags[2] == 1, 0.0, refs[0][last])
-    coefficients((1, HALO + 1), refs, lane)
-    coefficients((HALO + rows, span), refs, lane)
+    core = lax.axis_index("mem_2")
+    copies = [
+        pltpu.make_async_copy(source, near.at[k], sems.at[k]) for k, source in enumerate((low, high))
+    ]
+    for copy in copies:
+        copy.start()
 
     wide = lax.broadcasted_iota(jnp.int32, (span, LANES), 1)
     for u in range(4):
@@ -208,6 +199,43 @@
             for twin in range(2):
                 guess[u + 4 * odd, pl.ds(2 * l + twin, span, stride=8), :] = value
 
+    for copy in copies:
+        copy.wait()
+    matrix = splitting(256, 256)
+    lane = lax.broadcasted_iota(jnp.int32, (8, LANES), 1)
+
+    for u in range(low.shape[2] // 256):
+        cols = slice(u * 256, (u + 1) * 256)
+        for k, first in ((0, 0), (1, HALO + rows)):
+            source = near.at[k]
+            values = jnp.dot(
+                source[:16, :, cols].reshape(16 * HALO, 256).astype(BF16), matrix,
+                preferred_element_type=F32,
+            )
+            for m in range(4):
+                for l in range(levels):
+                    at = first * 16 + (m // 2) * 8 + 2 * l + m % 2
+                    at_row = (m * levels + l) * HALO
+                    for odd in range(2):
+                        member[u + 4 * odd, pl.ds(at, HALO, stride=16), :] = values[
+                            at_row:at_row + HALO, odd * LANES:(odd + 1) * LANES
+                        ]
+            values = exact_dot(source[16:, :, cols].reshape(12 * HALO, 256), matrix)
+            for a in range(3):
+                for l in range(levels):
+                    at_row = (a * levels + l) * HALO
+                    for odd in range(2):
+                        for twin in range(2):
+                            at = first * 8 + 2 * l + twin
+                            refs[a][u + 4 * odd, pl.ds(at, HALO, stride=8), :] = values[
+                                at_row:at_row + HALO, odd * LANES:(odd + 1) * LANES
+                            ]
+    for t in range(8):
+        last = (t, at8(HALO - 1), slice(None))
+        refs[0][last] = jnp.where(lax.axis_index("lat") == 0, 0.0, refs[0][last])
+    coefficients((1, HALO + 1), refs, lane)
+    coefficients((HALO + rows, span), refs, lane)
+
     def start(j, _):
         for t in range(8):
             scaled = step[t, at8(j), :] * guess[t, at8(j), :]
@@ -218,9 +246,9 @@
     lax.fori_loop(0, span, start, 0)
 
     def advance(source, target, first, count, finish):
-        def chunk(i, _):
-            for k in range(UNROLL):
-                j = first + i * UNROLL + k
+        def chunk(begin, length):
+            for k in range(length):
+                j = begin + k
                 for pair in range(2):
                     here = [source[t, at16(j, pair), :] for t in range(8)]
                     right, left = neighbours(here, lane)
@@ -235,7 +263,11 @@
                         target[t, at16(j, pair), :] = value
             return 0
 
-        lax.fori_loop(0, -(-count // UNROLL), chunk, 0)
+        count = -(-count // UNROLL) * UNROLL
+        whole = count // (2 * UNROLL)
+        lax.fori_loop(0, whole, lambda i, _: chunk(first + i * 2 * UNROLL, 2 * UNROLL), 0)
+        if count % (2 * UNROLL):
+            chunk(first + whole * 2 * UNROLL, UNROLL)
 
     for n in range(2 * SWEEP):
         advance(fields[n % 2], fields[1 - n % 2], n + 1, span - 2 * n - 2, n == SWEEP - 1)
@@ -275,34 +307,23 @@
     up = [(i, (i + 1) % size) for i in range(size)]
     down = [(j, i) for i, j in up]
     swap = [(0, 1), (1, 0)]
-    core = lax.axis_index("mem_2")
-    place = lax.axis_index("lat")
-    flags = jnp.stack([core, place == size - 1, place == 0]).astype(jnp.int32)
     vmem = pl.BlockSpec(memory_space=pltpu.VMEM)
-    smem = pl.BlockSpec(memory_space=pltpu.SMEM)
-
-    packed = pl.pallas_call(
-        pack_kernel,
-        out_shape=jax.ShapeDtypeStruct((rows, LANES), F32),
-        in_specs=[vmem], out_specs=vmem, name="pack",
-    )(gradient)
-    below = lax.ppermute(packed[rows - HALO:], "lat", up)
-    above = lax.ppermute(packed[:HALO], "lat", down)
-
-    def edge(block):
-        short = pl.BlockSpec((levels, HALO, width), lambda i: (0, block, 0))
-        return pl.pallas_call(
-            edge_kernel,
-            out_shape=jax.ShapeDtypeStruct((7 * levels, HALO, width), F32),
-            grid=(1,),
-            in_specs=[pl.BlockSpec((4, levels, HALO, width), lambda i: (0, 0, block, 0))] + [short] * 3,
-            out_specs=pl.BlockSpec((7 * levels, HALO, width), lambda i: (0, 0, 0)),
-            compiler_params=pltpu.CompilerParams(vmem_limit_bytes=8 * 2**20),
-            cost_estimate=pl.CostEstimate(flops=0, bytes_accessed=2 * 2**20, transcendentals=0),
-            name="edges",
-        )(perturb, k_north, k_east, scale)
-
-    top, bottom = edge(rows // HALO - 1), edge(0)
+    hbm = pl.BlockSpec(memory_space=pltpu.HBM)
+
+    rim = jax.ShapeDtypeStruct((HALO, LANES), F32)
+    edges = jax.ShapeDtypeStruct((7 * levels, HALO, width), F32)
+    packed, first, last, top, bottom = pl.pallas_call(
+        edge_kernel,
+        out_shape=[jax.ShapeDtypeStruct((rows, LANES), F32), rim, rim, edges, edges],
+        in_specs=[vmem] + [hbm] * 4, out_specs=[vmem] * 5,
+        scratch_shapes=[
+            pltpu.VMEM((2, 4, levels, HALO, width), BF16), pltpu.SemaphoreType.DMA((2, 4)),
+        ],
+        compiler_params=pltpu.CompilerParams(vmem_limit_bytes=CLOSED),
+        name="edges",
+    )(gradient, perturb, k_north, k_east, scale)
+    below = lax.ppermute(last, "lat", up)
+    above = lax.ppermute(first, "lat", down)
     low = lax.ppermute(top, "lat", up)
     high = lax.ppermute(bottom, "lat", down)
 
@@ -318,30 +339,32 @@
     prepare = pl.pallas_call(
         prepare_kernel,
         out_shape=[tall] + [short] * 9,
-        in_specs=[smem] + [vmem] * 4,
+        in_specs=[vmem] * 4,
         out_specs=[vmem] * 10,
-        compiler_params=pltpu.CompilerParams(vmem_limit_bytes=8 * 2**20),
+        compiler_params=pltpu.CompilerParams(vmem_limit_bytes=44 * 2**20),
         cost_estimate=pl.CostEstimate(flops=0, bytes_accessed=24 * 2**20, transcendentals=0),
         name="prepare",
     )
-    prepared = prepare(flags, perturb, k_north, k_east, scale)
+    prepared = prepare(perturb, k_north, k_east, scale)
 
     part = jax.ShapeDtypeStruct((chips, rows, LANES), F32)
     keep, send = pl.pallas_call(
         sweep_kernel,
         out_shape=[part, part] + [tall] + [short] * 9,
-        in_specs=[smem] + [vmem] * 14,
+        in_specs=[hbm] * 2 + [vmem] * 12,
         out_specs=[vmem] * 12,
-        input_output_aliases={5 + k: 2 + k for k in range(10)},
+        input_output_aliases={4 + k: 2 + k for k in range(10)},
         scratch_shapes=[
             tall,
             tall,
             pltpu.VMEM((8, span * 8, LANES), F32),
             pltpu.VMEM((8, rows * 8, LANES), F32),
+            pltpu.VMEM((2, 7 * levels, HALO, width), F32),
+            pltpu.SemaphoreType.DMA((2,)),
         ],
         compiler_params=pltpu.CompilerParams(vmem_limit_bytes=18 * 2**20),
         name="sweeps",
-    )(flags, low, high, mine, other, *prepared)[:2]
+    )(low, high, mine, other, *prepared)[:2]
 
     merged = keep + lax.ppermute(send, "mem_2", swap)
     parts = lax.all_to_all(merged, CHIP, 0, 0, tiled=True)
@@ -349,7 +372,9 @@
     return pl.pallas_call(
         lambda p, o: finish_kernel(count, p, o),
         out_shape=jax.ShapeDtypeStruct((levels, rows, GROUP), F32),
-        in_specs=[vmem], out_specs=vmem, name="finish",
+        in_specs=[vmem], out_specs=vmem,
+        compiler_params=pltpu.CompilerParams(vmem_limit_bytes=4 * 2**20),
+        name="finish",
     )(parts)
 
 

time: 93.8 us -> 82.6 us (0.88)
  Pallas kernels: 30.1 us -> 24.6 us
  local copies, waits for them, and re-layouts: 5.1 us -> 0.03 us
    unnamed x16 -> x0, local copies, waits for them, and re-layouts: 4.36 us -> none
    pallas_call x1, Pallas kernels: 19.8 us -> 15.8 us  [shards(): pl.pallas_call(sweep_kernel, out_shape=[part, part] + [tall] + [short] *...]
    ppermute x1, starting transfers between devices: 0.01 us -> 2.53 us  [shards(): low = lax.ppermute(top, 'lat', up)]
    ppermute x1, starting transfers between devices: 6.47 us -> 4.03 us  [shards(): high = lax.ppermute(bottom, 'lat', down)]
    pallas_call x1, Pallas kernels: 1.81 us -> 0.87 us  [shards(): pl.pallas_call(lambda p, o: finish_kernel(count, p, o), out_shape=jax.Sha...]
    pallas_call x4 -> x2, Pallas kernels: 8.54 us -> 7.9 us  [the longest x1 4.39 us: shards(): prepared = prepare(perturb, k_north, k_east, scale)]
  transfers between devices with their start and end apart: 6 -> 6, of which waited for: 2 -> 2; matrix products, arithmetic and copies ran while one was open for 2% -> 1% of each run, Pallas kernels for 8% -> 5%
where the time goes in v3:
time: 82.6 us; the launch traced here: 82.2 us
  blocking collectives  25.7 us (31%)
  Pallas kernels  24.6 us (30%)
  waiting for transfers between devices  19.1 us (23%)
  starting transfers between devices  12 us (15%)
    ppermute x1, waiting for transfers between devices, shards(): below = lax.ppermute(last, 'lat', up)  17.6 us
    pallas_call x1, Pallas kernels, shards(): pl.pallas_call(sweep_kernel, out_shape=[part, part] + [tall] + [short] *...  15.8 us
    all_to_all x1, blocking collectives, shards(): mine = lax.all_to_all(spread, CHIP, 0, 0, tiled=True)  14.7 us
    all_to_all x1, blocking collectives, shards(): parts = lax.all_to_all(merged, CHIP, 0, 0, tiled=True)  11 us
    pallas_call x1, Pallas kernels, shards(): prepared = prepare(perturb, k_north, k_east, scale)  4.39 us
    ppermute x1, starting transfers between devices, shards(): high = lax.ppermute(bottom, 'lat', down)  4.03 us
    pallas_call x1, Pallas kernels, shards(): pl.pallas_call(edge_kernel, out_shape=[jax.ShapeDtypeStruct((rows, LANES)...  3.51 us
    ppermute x1, starting transfers between devices, shards(): above = lax.ppermute(first, 'lat', down)  2.67 us
  transfers between devices with their start and end apart: 6, of which 2 were waited for; matrix products, arithmetic and copies ran while one was open for 1% of the time, Pallas kernels for 5%

profile of v3, /device:TPU:1, one launch (start us, length us, event | category | flops | bytes accessed | tf_op | source)
XLA Modules:
  0.0 82.2 jit_solution(3587421972431632856)
XLA Ops:
  0.0 3.5 %edges.1 = (f32[32,128]{1,0:T(8,128)}, f32[8,128]{1,0:T(8,128)}, f32[8,128]{1,0:T(8,128)}, f32[28,8,1024]{2,1,0:T(8,128)}, f32[28,8,1024]{2,1,0:T(8,128)}) custom-call(f32[4,32,32]{2,1,0:T(8,128)} %gradient.1, bf16[4,4,32,1024]{3,2,1,0:T(8,128)(2,1)} %perturb.3, f32[4,32,1024]{2,1,0:T(8,128)} %k_north.3, f32[4,32,1024]{2,1,0:T(8,128)} %k_east.3, ...), custom_call_target="tpu_custom_call" | custom-call | tf_op jit(solution)/shard_map/edges/pallas_call | solution.py:315
  3.5 2.5 %collective-permute-start = (f32[28,8,1024]{2,1,0:T(8,128)}, f32[28,8,1024]{2,1,0:T(8,128)S(1)}, u32[]{:S(2)}, u32[]{:S(2)}) collective-permute-start(f32[28,8,1024]{2,1,0:T(8,128)} %get-tuple-element.22), channel_id=1, source_target_pairs={{0,1},{1,2},{2,3},{3,4},{4,5},{5,6},{6,7},{7,0},{8,9},{9,10},{10,1... | collective-permute-start | bytes 2752520 | tf_op jit(solution)/shard_map/ppermute | solution.py:327
  6.1 4.0 %collective-permute-start.1 = (f32[28,8,1024]{2,1,0:T(8,128)}, f32[28,8,1024]{2,1,0:T(8,128)}, u32[]{:S(2)}, u32[]{:S(2)}) collective-permute-start(f32[28,8,1024]{2,1,0:T(8,128)} %get-tuple-element.23), channel_id=1, source_target_pairs={{1,0},{2,1},{3,2},{4,3},{5,4},{6,5},{7,6},{0,7},{9,8},{10,9},{11,1... | collective-permute-start | bytes 2752520 | tf_op jit(solution)/shard_map/ppermute | solution.py:328
  10.1 0.0 collective-permute-start.2
  10.1 2.7 %collective-permute-start.3 = (f32[8,128]{1,0:T(8,128)}, f32[8,128]{1,0:T(8,128)S(1)}, u32[]{:S(2)}, u32[]{:S(2)}) collective-permute-start(f32[8,128]{1,0:T(8,128)} %get-tuple-element.26), channel_id=1, source_target_pairs={{1,0},{2,1},{3,2},{4,3},{5,4},{6,5},{7,6},{0,7},{9,8},{10,9},{11,1... | collective-permute-start | bytes 12296 | tf_op jit(solution)/shard_map/ppermute | solution.py:326
  12.8 17.6 %collective-permute-done.2 = f32[8,128]{1,0:T(8,128)S(1)} collective-permute-done((f32[8,128]{1,0:T(8,128)}, f32[8,128]{1,0:T(8,128)S(1)}, u32[]{:S(2)}, u32[]{:S(2)}) %collective-permute-start.2) | collective-permute-done | bytes 4128 | tf_op jit(solution)/shard_map/ppermute | solution.py:325
  30.3 0.0 collective-permute-done.3
  30.3 0.7 pad_maximum_fusion
  31.1 14.7 %all_to_all.10.mine = f32[16,48,128]{2,1,0:T(8,128)S(1)} all-to-all(f32[16,48,128]{2,1,0:T(8,128)S(1)} %broadcast_in_dim.2), channel_id=1, replica_groups=mesh['mem_0'=4,'mem_1'=4,'mem_2'=2,'lat'=8] {'mem_0','mem_1'}, dimensions={0} | all-to-all | bytes 786432 | tf_op jit(solution)/shard_map/all_to_all | solution.py:333
  45.8 2.6 %collective-permute-start.4 = (f32[16,48,128]{2,1,0:T(8,128)S(1)}, f32[16,48,128]{2,1,0:T(8,128)S(1)}, u32[]{:S(2)}, u32[]{:S(2)}) collective-permute-start(f32[16,48,128]{2,1,0:T(8,128)S(1)} %all_to_all.10.mine), channel_id=1, source_target_pairs={{0,8},{8,0},{1,9},{9,1},{2,10},{10,2},{3,11},{11,3},{4,12},{12,4},... | collective-permute-start | bytes 1179656 | tf_op jit(solution)/shard_map/ppermute | solution.py:334
  48.4 4.4 %prepare.1 = (f32[8,832,128]{2,1,0:T(8,128)S(1)}, f32[8,416,128]{2,1,0:T(8,128)S(1)}, f32[8,416,128]{2,1,0:T(8,128)S(1)}, f32[8,416,128]{2,1,0:T(8,128)S(1)}, f3...) custom-call(bf16[4,4,32,1024]{3,2,1,0:T(8,128)(2,1)} %perturb.3, ...), custom_call_target="tpu_custom_call" | custom-call | bytes 25165824 | tf_op jit(solution)/shard_map/prepare/pallas_call | solution.py:348
  52.8 0.0 collective-permute-done.4.other
  52.8 0.0 collective-permute-done.low
  52.9 0.0 collective-permute-done.1.high
  52.9 15.8 %sweeps.1 = (f32[16,32,128]{2,1,0:T(8,128)S(1)}, f32[16,32,128]{2,1,0:T(8,128)S(1)}, f32[8,832,128]{2,1,0:T(8,128)S(1)}, f32[8,416,128]{2,1,0:T(8,128)S(1)}, f32...) custom-call(f32[28,8,1024]{2,1,0:T(8,128)S(1)} %collective-permute-d, ...), custom_call_target="tpu_custom_call", output_to_operand_aliasing={{2}: (4, {}), {3}: (5, {}), {4}: (6, {}), {5}: (7, {}), {6}... | custom-call | tf_op jit(solution)/shard_map/sweeps/pallas_call | solution.py:351
  68.7 0.1 collective-permute-start.5
  68.8 1.5 %collective-permute-done.5 = f32[16,32,128]{2,1,0:T(8,128)S(1)} collective-permute-done((f32[16,32,128]{2,1,0:T(8,128)S(1)}, f32[16,32,128]{2,1,0:T(8,128)S(1)}, u32[]{:S(2)}, u32[]{:S(2)}) %collective-permute-start.5) | collective-permute-done | bytes 262176 | tf_op jit(solution)/shard_map/ppermute | solution.py:369
  70.3 11.0 %all_to_all.11.p = f32[16,32,128]{2,1,0:T(8,128)S(1)} all-to-all(f32[16,32,128]{2,1,0:T(8,128)S(1)} %add.3), channel_id=1, replica_groups=mesh['mem_0'=4,'mem_1'=4,'mem_2'=2,'lat'=8] {'mem_0','mem_1'}, dimensions={0} | all-to-all | bytes 524288 | tf_op jit(solution)/shard_map/all_to_all | solution.py:370
  81.4 0.9 %finish.1 = f32[4,32,32]{2,1,0:T(8,128)} custom-call(f32[16,32,128]{2,1,0:T(8,128)S(1)} %all_to_all.11.p), custom_call_target="tpu_custom_call" | custom-call | tf_op jit(solution)/shard_map/finish/pallas_call | solution.py:372
  (2 shorter events, 0.1 us)
Async XLA Ops:
  3.5 49.3 %collective-permute-start = (f32[28,8,1024]{2,1,0:T(8,128)}, f32[28,8,1024]{2,1,0:T(8,128)S(1)}, u32[]{:S(2)}, u32[]{:S(2)}) collective-permute-start(f32[28,8,1024]{2,1,0:T(8,128)} %get-tuple-element.22), channel_id=1, source_target_pairs={{0,1},{1,2},{2,3},{3,4},{4,5},{5,6},{6,7},{7,0},{8,9},{9,10},{10,1... | collective-permute-start | bytes 2752520 | tf_op jit(solution)/shard_map/ppermute | solution.py:327
  6.1 46.8 %collective-permute-start.1 = (f32[28,8,1024]{2,1,0:T(8,128)}, f32[28,8,1024]{2,1,0:T(8,128)}, u32[]{:S(2)}, u32[]{:S(2)}) collective-permute-start(f32[28,8,1024]{2,1,0:T(8,128)} %get-tuple-element.23), channel_id=1, source_target_pairs={{1,0},{2,1},{3,2},{4,3},{5,4},{6,5},{7,6},{0,7},{9,8},{10,9},{11,1... | collective-permute-start | bytes 2752520 | tf_op jit(solution)/shard_map/ppermute | solution.py:328
  10.1 20.3 %collective-permute-start.2 = (f32[8,128]{1,0:T(8,128)}, f32[8,128]{1,0:T(8,128)S(1)}, u32[]{:S(2)}, u32[]{:S(2)}) collective-permute-start(f32[8,128]{1,0:T(8,128)} %get-tuple-element.24), channel_id=1, source_target_pairs={{0,1},{1,2},{2,3},{3,4},{4,5},{5,6},{6,7},{7,0},{8,9},{9,10},{10,1... | collective-permute-start | bytes 12296 | tf_op jit(solution)/shard_map/ppermute | solution.py:325
  10.1 20.3 %collective-permute-start.3 = (f32[8,128]{1,0:T(8,128)}, f32[8,128]{1,0:T(8,128)S(1)}, u32[]{:S(2)}, u32[]{:S(2)}) collective-permute-start(f32[8,128]{1,0:T(8,128)} %get-tuple-element.26), channel_id=1, source_target_pairs={{1,0},{2,1},{3,2},{4,3},{5,4},{6,5},{7,6},{0,7},{9,8},{10,9},{11,1... | collective-permute-start | bytes 12296 | tf_op jit(solution)/shard_map/ppermute | solution.py:326
  45.8 7.0 %collective-permute-start.4 = (f32[16,48,128]{2,1,0:T(8,128)S(1)}, f32[16,48,128]{2,1,0:T(8,128)S(1)}, u32[]{:S(2)}, u32[]{:S(2)}) collective-permute-start(f32[16,48,128]{2,1,0:T(8,128)S(1)} %all_to_all.10.mine), channel_id=1, source_target_pairs={{0,8},{8,0},{1,9},{9,1},{2,10},{10,2},{3,11},{11,3},{4,12},{12,4},... | collective-permute-start | bytes 1179656 | tf_op jit(solution)/shard_map/ppermute | solution.py:334
  68.7 1.6 %collective-permute-start.5 = (f32[16,32,128]{2,1,0:T(8,128)S(1)}, f32[16,32,128]{2,1,0:T(8,128)S(1)}, u32[]{:S(2)}, u32[]{:S(2)}) collective-permute-start(f32[16,32,128]{2,1,0:T(8,128)S(1)} %get-tuple-element.38), channel_id=1, source_target_pairs={{0,8},{8,0},{1,9},{9,1},{2,10},{10,2},{3,11},{11,3},{4,12},{12,4},... | collective-permute-start | bytes 786440 | tf_op jit(solution)/shard_map/ppermute | solution.py:369

commit v4 on v3

--- a/solution.py
+++ b/solution.py
@@ -73,32 +73,46 @@
     return odd + east, west + even
 
 
-def edge_kernel(gradient, perturb, k_north, k_east, scale,
-                packed, first, last, top, bottom, narrow, sems):
+def edge_kernel(gradient, perturb, k_north, k_east, scale, packed, first, last, top, bottom,
+                block, narrow, wide, arrive, leave):
     rows = perturb.shape[2]
-    copies = []
+    load = pltpu.make_async_copy(gradient, block, arrive.at[2, 0])
+    load.start()
+    inward, outward = [], []
     for side, (out, start) in enumerate(((top, rows - HALO), (bottom, 0))):
         at = pl.ds(start, HALO)
-        copies.append(pltpu.make_async_copy(
-            perturb.at[:, :, at, :], narrow.at[side], sems.at[side, 0]
-        ))
-        for a, ref in enumerate((k_north, k_east, scale)):
-            copies.append(pltpu.make_async_copy(
-                ref.at[:, at, :], out.at[pl.ds(16 + 4 * a, 4)], sems.at[side, 1 + a]
-            ))
-    for copy in copies:
-        copy.start()
-    joined = jnp.concatenate([gradient[l] for l in range(gradient.shape[0])], axis=1)
+        inward.append([
+            pltpu.make_async_copy(ref.at[:, at, :], wide.at[side, pl.ds(16 + 4 * a, 4)],
+                                  arrive.at[side, a])
+            for a, ref in enumerate((k_north, k_east, scale))
+        ] + [pltpu.make_async_copy(perturb.at[:, :, at, :], narrow.at[side], arrive.at[side, 3])])
+        outward.append([
+            pltpu.make_async_copy(wide.at[side, pl.ds(k, 4)], out.at[pl.ds(k, 4)],
+                                  leave.at[side, k // 4])
+            for k in range(0, 28, 4)
+        ])
+    for side in range(2):
+        for copy in inward[side]:
+            copy.start()
+    load.wait()
+    joined = jnp.concatenate([block[l] for l in range(block.shape[0])], axis=1)
     value = exact_dot(joined, splitting(LANES, GROUP))
     packed[...] = value
     first[...] = value[:HALO]
     last[...] = value[-HALO:]
-    for copy in copies:
-        copy.wait()
-    for side, out in enumerate((top, bottom)):
+    for side in range(2):
+        for a in range(3):
+            inward[side][a].wait()
+            outward[side][4 + a].start()
+    for side in range(2):
+        inward[side][3].wait()
         for m in range(4):
             for l in range(4):
-                out[4 * m + l] = narrow[side, m, l].astype(F32)
+                wide[side, 4 * m + l] = narrow[side, m, l].astype(F32)
+            outward[side][m].start()
+    for side in range(2):
+        for copy in outward[side]:
+            copy.wait()
 
 
 def finish_kernel(count, parts, out):
@@ -245,10 +259,11 @@
 
     lax.fori_loop(0, span, start, 0)
 
-    def advance(source, target, first, count, finish):
+    def advance(source, target, first, count, finish, last):
         def chunk(begin, length):
             for k in range(length):
                 j = begin + k
+                terms = [None] * 8
                 for pair in range(2):
                     here = [source[t, at16(j, pair), :] for t in range(8)]
                     right, left = neighbours(here, lane)
@@ -260,7 +275,14 @@
                         value += side
                         if finish:
                             value = value * inverse[t, at8(j), :]
-                        target[t, at16(j, pair), :] = value
+                        if not last:
+                            target[t, at16(j, pair), :] = value
+                        else:
+                            term = member[t, at16(j, pair), :] * value
+                            terms[t] = term if pair == 0 else terms[t] + term
+                if last:
+                    for t in range(8):
+                        total[t, at8(j - HALO), :] = terms[t]
             return 0
 
         count = -(-count // UNROLL) * UNROLL
@@ -270,20 +292,8 @@
             chunk(first + whole * 2 * UNROLL, UNROLL)
 
     for n in range(2 * SWEEP):
-        advance(fields[n % 2], fields[1 - n % 2], n + 1, span - 2 * n - 2, n == SWEEP - 1)
-    result = fields[0]
-
-    def gather(j, _):
-        for t in range(8):
-            value = None
-            for pair in range(2):
-                term = member[t, at16(j + HALO, pair), :] * result[t, at16(j + HALO, pair), :]
-                value = term if value is None else value + term
-            total[t, at8(j), :] = value
-        return 0
-
-    lax.fori_loop(0, rows, gather, 0)
-
+        advance(fields[n % 2], fields[1 - n % 2], n + 1, span - 2 * n - 2,
+                n == SWEEP - 1, n == 2 * SWEEP - 1)
     wide = lax.broadcasted_iota(jnp.int32, (rows, LANES), 1)
     for u in range(4):
         sums = []
@@ -315,9 +325,13 @@
     packed, first, last, top, bottom = pl.pallas_call(
         edge_kernel,
         out_shape=[jax.ShapeDtypeStruct((rows, LANES), F32), rim, rim, edges, edges],
-        in_specs=[vmem] + [hbm] * 4, out_specs=[vmem] * 5,
+        in_specs=[hbm] * 5, out_specs=[vmem] * 3 + [hbm] * 2,
         scratch_shapes=[
-            pltpu.VMEM((2, 4, levels, HALO, width), BF16), pltpu.SemaphoreType.DMA((2, 4)),
+            pltpu.VMEM(gradient.shape, F32),
+            pltpu.VMEM((2, 4, levels, HALO, width), BF16),
+            pltpu.VMEM((2, 7 * levels, HALO, width), F32),
+            pltpu.SemaphoreType.DMA((3, 4)),
+            pltpu.SemaphoreType.DMA((2, 7)),
         ],
         compiler_params=pltpu.CompilerParams(vmem_limit_bytes=CLOSED),
         name="edges",

time: 82.6 us -> 81.9 us (level)
  no operation moved by 1% of the time
where the time goes in v4:
time: 81.9 us; the launch traced here: 81.6 us
  blocking collectives  25.7 us (31%)
  Pallas kernels  23.9 us (29%)
  waiting for transfers between devices  19.1 us (23%)
  starting transfers between devices  12 us (15%)
    ppermute x1, waiting for transfers between devices, shards(): below = lax.ppermute(last, 'lat', up)  17.6 us
    pallas_call x1, Pallas kernels, shards(): pl.pallas_call(sweep_kernel, out_shape=[part, part] + [tall] + [short] *...  15.5 us
    all_to_all x1, blocking collectives, shards(): mine = lax.all_to_all(spread, CHIP, 0, 0, tiled=True)  14.7 us
    all_to_all x1, blocking collectives, shards(): parts = lax.all_to_all(merged, CHIP, 0, 0, tiled=True)  11 us
    pallas_call x1, Pallas kernels, shards(): prepared = prepare(perturb, k_north, k_east, scale)  4.39 us
    ppermute x1, starting transfers between devices, shards(): high = lax.ppermute(bottom, 'lat', down)  4.03 us
    pallas_call x1, Pallas kernels, shards(): pl.pallas_call(edge_kernel, out_shape=[jax.ShapeDtypeStruct((rows, LANES)...  3.16 us
    ppermute x1, starting transfers between devices, shards(): above = lax.ppermute(first, 'lat', down)  2.67 us
  transfers between devices with their start and end apart: 6, of which 2 were waited for; matrix products, arithmetic and copies ran while one was open for 1% of the time, Pallas kernels for 5%

profile of v4, /device:TPU:1, one launch (start us, length us, event | category | flops | bytes accessed | tf_op | source)
XLA Modules:
  0.0 81.6 jit_solution(14277049430798889758)
XLA Ops:
  0.0 3.2 %edges.1 = (f32[32,128]{1,0:T(8,128)}, f32[8,128]{1,0:T(8,128)}, f32[8,128]{1,0:T(8,128)}, f32[28,8,1024]{2,1,0:T(8,128)}, f32[28,8,1024]{2,1,0:T(8,128)}) custom-call(f32[4,32,32]{2,1,0:T(8,128)} %gradient.1, bf16[4,4,32,1024]{3,2,1,0:T(8,128)(2,1)} %perturb.3, f32[4,32,1024]{2,1,0:T(8,128)} %k_north.3, f32[4,32,1024]{2,1,0:T(8,128)} %k_east.3, ...), custom_call_target="tpu_custom_call" | custom-call | tf_op jit(solution)/shard_map/edges/pallas_call | solution.py:325
  3.2 2.5 %collective-permute-start = (f32[28,8,1024]{2,1,0:T(8,128)}, f32[28,8,1024]{2,1,0:T(8,128)S(1)}, u32[]{:S(2)}, u32[]{:S(2)}) collective-permute-start(f32[28,8,1024]{2,1,0:T(8,128)} %get-tuple-element.22), channel_id=1, source_target_pairs={{0,1},{1,2},{2,3},{3,4},{4,5},{5,6},{6,7},{7,0},{8,9},{9,10},{10,1... | collective-permute-start | bytes 2752520 | tf_op jit(solution)/shard_map/ppermute | solution.py:341
  5.7 4.0 %collective-permute-start.1 = (f32[28,8,1024]{2,1,0:T(8,128)}, f32[28,8,1024]{2,1,0:T(8,128)}, u32[]{:S(2)}, u32[]{:S(2)}) collective-permute-start(f32[28,8,1024]{2,1,0:T(8,128)} %get-tuple-element.23), channel_id=1, source_target_pairs={{1,0},{2,1},{3,2},{4,3},{5,4},{6,5},{7,6},{0,7},{9,8},{10,9},{11,1... | collective-permute-start | bytes 2752520 | tf_op jit(solution)/shard_map/ppermute | solution.py:342
  9.7 0.0 collective-permute-start.2
  9.7 2.7 %collective-permute-start.3 = (f32[8,128]{1,0:T(8,128)}, f32[8,128]{1,0:T(8,128)S(1)}, u32[]{:S(2)}, u32[]{:S(2)}) collective-permute-start(f32[8,128]{1,0:T(8,128)} %get-tuple-element.26), channel_id=1, source_target_pairs={{1,0},{2,1},{3,2},{4,3},{5,4},{6,5},{7,6},{0,7},{9,8},{10,9},{11,1... | collective-permute-start | bytes 12296 | tf_op jit(solution)/shard_map/ppermute | solution.py:340
  12.4 17.6 %collective-permute-done.2 = f32[8,128]{1,0:T(8,128)S(1)} collective-permute-done((f32[8,128]{1,0:T(8,128)}, f32[8,128]{1,0:T(8,128)S(1)}, u32[]{:S(2)}, u32[]{:S(2)}) %collective-permute-start.2) | collective-permute-done | bytes 4128 | tf_op jit(solution)/shard_map/ppermute | solution.py:339
  30.0 0.0 collective-permute-done.3
  30.0 0.7 pad_maximum_fusion
  30.8 14.7 %all_to_all.10.mine = f32[16,48,128]{2,1,0:T(8,128)S(1)} all-to-all(f32[16,48,128]{2,1,0:T(8,128)S(1)} %broadcast_in_dim.2), channel_id=1, replica_groups=mesh['mem_0'=4,'mem_1'=4,'mem_2'=2,'lat'=8] {'mem_0','mem_1'}, dimensions={0} | all-to-all | bytes 786432 | tf_op jit(solution)/shard_map/all_to_all | solution.py:347
  45.4 2.6 %collective-permute-start.4 = (f32[16,48,128]{2,1,0:T(8,128)S(1)}, f32[16,48,128]{2,1,0:T(8,128)S(1)}, u32[]{:S(2)}, u32[]{:S(2)}) collective-permute-start(f32[16,48,128]{2,1,0:T(8,128)S(1)} %all_to_all.10.mine), channel_id=1, source_target_pairs={{0,8},{8,0},{1,9},{9,1},{2,10},{10,2},{3,11},{11,3},{4,12},{12,4},... | collective-permute-start | bytes 1179656 | tf_op jit(solution)/shard_map/ppermute | solution.py:348
  48.1 4.4 %prepare.1 = (f32[8,832,128]{2,1,0:T(8,128)S(1)}, f32[8,416,128]{2,1,0:T(8,128)S(1)}, f32[8,416,128]{2,1,0:T(8,128)S(1)}, f32[8,416,128]{2,1,0:T(8,128)S(1)}, f3...) custom-call(bf16[4,4,32,1024]{3,2,1,0:T(8,128)(2,1)} %perturb.3, ...), custom_call_target="tpu_custom_call" | custom-call | bytes 25165824 | tf_op jit(solution)/shard_map/prepare/pallas_call | solution.py:362
  52.5 0.0 collective-permute-done.4.other
  52.5 0.0 collective-permute-done.low
  52.5 0.0 collective-permute-done.1.high
  52.5 15.5 %sweeps.1 = (f32[16,32,128]{2,1,0:T(8,128)S(1)}, f32[16,32,128]{2,1,0:T(8,128)S(1)}, f32[8,832,128]{2,1,0:T(8,128)S(1)}, f32[8,416,128]{2,1,0:T(8,128)S(1)}, f32...) custom-call(f32[28,8,1024]{2,1,0:T(8,128)S(1)} %collective-permute-d, ...), custom_call_target="tpu_custom_call", output_to_operand_aliasing={{2}: (4, {}), {3}: (5, {}), {4}: (6, {}), {5}: (7, {}), {6}... | custom-call | tf_op jit(solution)/shard_map/sweeps/pallas_call | solution.py:365
  68.0 0.1 collective-permute-start.5
  68.1 1.5 %collective-permute-done.5 = f32[16,32,128]{2,1,0:T(8,128)S(1)} collective-permute-done((f32[16,32,128]{2,1,0:T(8,128)S(1)}, f32[16,32,128]{2,1,0:T(8,128)S(1)}, u32[]{:S(2)}, u32[]{:S(2)}) %collective-permute-start.5) | collective-permute-done | bytes 262176 | tf_op jit(solution)/shard_map/ppermute | solution.py:383
  69.7 11.0 %all_to_all.11.p = f32[16,32,128]{2,1,0:T(8,128)S(1)} all-to-all(f32[16,32,128]{2,1,0:T(8,128)S(1)} %add.3), channel_id=1, replica_groups=mesh['mem_0'=4,'mem_1'=4,'mem_2'=2,'lat'=8] {'mem_0','mem_1'}, dimensions={0} | all-to-all | bytes 524288 | tf_op jit(solution)/shard_map/all_to_all | solution.py:384
  80.7 0.9 %finish.1 = f32[4,32,32]{2,1,0:T(8,128)} custom-call(f32[16,32,128]{2,1,0:T(8,128)S(1)} %all_to_all.11.p), custom_call_target="tpu_custom_call" | custom-call | tf_op jit(solution)/shard_map/finish/pallas_call | solution.py:386
  (2 shorter events, 0.1 us)
Async XLA Ops:
  3.2 49.3 %collective-permute-start = (f32[28,8,1024]{2,1,0:T(8,128)}, f32[28,8,1024]{2,1,0:T(8,128)S(1)}, u32[]{:S(2)}, u32[]{:S(2)}) collective-permute-start(f32[28,8,1024]{2,1,0:T(8,128)} %get-tuple-element.22), channel_id=1, source_target_pairs={{0,1},{1,2},{2,3},{3,4},{4,5},{5,6},{6,7},{7,0},{8,9},{9,10},{10,1... | collective-permute-start | bytes 2752520 | tf_op jit(solution)/shard_map/ppermute | solution.py:341
  5.7 46.8 %collective-permute-start.1 = (f32[28,8,1024]{2,1,0:T(8,128)}, f32[28,8,1024]{2,1,0:T(8,128)}, u32[]{:S(2)}, u32[]{:S(2)}) collective-permute-start(f32[28,8,1024]{2,1,0:T(8,128)} %get-tuple-element.23), channel_id=1, source_target_pairs={{1,0},{2,1},{3,2},{4,3},{5,4},{6,5},{7,6},{0,7},{9,8},{10,9},{11,1... | collective-permute-start | bytes 2752520 | tf_op jit(solution)/shard_map/ppermute | solution.py:342
  9.7 20.3 %collective-permute-start.2 = (f32[8,128]{1,0:T(8,128)}, f32[8,128]{1,0:T(8,128)S(1)}, u32[]{:S(2)}, u32[]{:S(2)}) collective-permute-start(f32[8,128]{1,0:T(8,128)} %get-tuple-element.24), channel_id=1, source_target_pairs={{0,1},{1,2},{2,3},{3,4},{4,5},{5,6},{6,7},{7,0},{8,9},{9,10},{10,1... | collective-permute-start | bytes 12296 | tf_op jit(solution)/shard_map/ppermute | solution.py:339
  9.7 20.3 %collective-permute-start.3 = (f32[8,128]{1,0:T(8,128)}, f32[8,128]{1,0:T(8,128)S(1)}, u32[]{:S(2)}, u32[]{:S(2)}) collective-permute-start(f32[8,128]{1,0:T(8,128)} %get-tuple-element.26), channel_id=1, source_target_pairs={{1,0},{2,1},{3,2},{4,3},{5,4},{6,5},{7,6},{0,7},{9,8},{10,9},{11,1... | collective-permute-start | bytes 12296 | tf_op jit(solution)/shard_map/ppermute | solution.py:340
  45.4 7.0 %collective-permute-start.4 = (f32[16,48,128]{2,1,0:T(8,128)S(1)}, f32[16,48,128]{2,1,0:T(8,128)S(1)}, u32[]{:S(2)}, u32[]{:S(2)}) collective-permute-start(f32[16,48,128]{2,1,0:T(8,128)S(1)} %all_to_all.10.mine), channel_id=1, source_target_pairs={{0,8},{8,0},{1,9},{9,1},{2,10},{10,2},{3,11},{11,3},{4,12},{12,4},... | collective-permute-start | bytes 1179656 | tf_op jit(solution)/shard_map/ppermute | solution.py:348
  68.0 1.6 %collective-permute-start.5 = (f32[16,32,128]{2,1,0:T(8,128)S(1)}, f32[16,32,128]{2,1,0:T(8,128)S(1)}, u32[]{:S(2)}, u32[]{:S(2)}) collective-permute-start(f32[16,32,128]{2,1,0:T(8,128)S(1)} %get-tuple-element.38), channel_id=1, source_target_pairs={{0,8},{8,0},{1,9},{9,1},{2,10},{10,2},{3,11},{11,3},{4,12},{12,4},... | collective-permute-start | bytes 786440 | tf_op jit(solution)/shard_map/ppermute | solution.py:383

commit v5 on v4

--- a/solution.py
+++ b/solution.py
@@ -154,14 +154,30 @@
     lax.fori_loop(0, (rows[1] - rows[0]) // UNROLL, chunk, 0)
 
 
-def prepare_kernel(perturb, k_north, k_east, scale, member, *refs):
-    levels, rows, width = k_north.shape
+def prepare_kernel(perturb_all, north_all, east_all, scale_all, member, *args):
+    refs, (perturb, faces, sems) = args[:9], args[9:]
+    levels, rows, width = north_all.shape
     north, east, step = refs[:3]
+    halves = [
+        pltpu.make_async_copy(
+            perturb_all.at[:, :, :, pl.ds(k * width // 4, width // 4)],
+            perturb.at[:, :, :, pl.ds(k * width // 4, width // 4)], sems.at[k],
+        )
+        for k in range(4)
+    ]
+    copies = [
+        pltpu.make_async_copy(source, faces.at[a], sems.at[4 + a])
+        for a, source in enumerate((north_all, east_all, scale_all))
+    ]
+    for copy in halves + copies:
+        copy.start()
+    k_north, k_east, scale = (faces.at[a] for a in range(3))
     matrix = splitting(256, 256)
     row = lax.broadcasted_iota(jnp.int32, (rows, 256), 0)
     edge = (row == rows - 1) & (lax.axis_index("lat") == lax.axis_size("lat") - 1)
     for u in range(width // 256):
         cols = slice(u * 256, (u + 1) * 256)
+        halves[u].wait()
         for m in range(4):
             values = jnp.dot(
                 perturb[m, :, :, cols].reshape(levels * rows, 256), matrix,
@@ -173,6 +189,10 @@
                     member[u + 4 * odd, pl.ds(at, rows, stride=16), :] = values[
                         l * rows:(l + 1) * rows, odd * LANES:(odd + 1) * LANES
                     ]
+    for copy in copies:
+        copy.wait()
+    for u in range(width // 256):
+        cols = slice(u * 256, (u + 1) * 256)
         for ref, source in ((north, k_north), (east, k_east), (step, scale)):
             parts = [source[l, :, cols] for l in range(levels)]
             if ref is north:
@@ -202,6 +222,8 @@
     for copy in copies:
         copy.start()
 
+    for copy in copies:
+        copy.wait()
     wide = lax.broadcasted_iota(jnp.int32, (span, LANES), 1)
     for u in range(4):
         blocks = []
@@ -213,8 +235,6 @@
             for twin in range(2):
                 guess[u + 4 * odd, pl.ds(2 * l + twin, span, stride=8), :] = value
 
-    for copy in copies:
-        copy.wait()
     matrix = splitting(256, 256)
     lane = lax.broadcasted_iota(jnp.int32, (8, LANES), 1)
 
@@ -250,14 +270,16 @@
     coefficients((1, HALO + 1), refs, lane)
     coefficients((HALO + rows, span), refs, lane)
 
-    def start(j, _):
-        for t in range(8):
-            scaled = step[t, at8(j), :] * guess[t, at8(j), :]
-            for pair in range(2):
-                fields[0][t, at16(j, pair), :] = member[t, at16(j, pair), :] * scaled
+    def start(i, _):
+        for k in range(UNROLL):
+            j = i * UNROLL + k
+            for t in range(8):
+                scaled = step[t, at8(j), :] * guess[t, at8(j), :]
+                for pair in range(2):
+                    fields[0][t, at16(j, pair), :] = member[t, at16(j, pair), :] * scaled
         return 0
 
-    lax.fori_loop(0, span, start, 0)
+    lax.fori_loop(0, span // UNROLL, start, 0)
 
     def advance(source, target, first, count, finish, last):
         def chunk(begin, length):
@@ -285,11 +307,10 @@
                         total[t, at8(j - HALO), :] = terms[t]
             return 0
 
-        count = -(-count // UNROLL) * UNROLL
         whole = count // (2 * UNROLL)
         lax.fori_loop(0, whole, lambda i, _: chunk(first + i * 2 * UNROLL, 2 * UNROLL), 0)
         if count % (2 * UNROLL):
-            chunk(first + whole * 2 * UNROLL, UNROLL)
+            chunk(first + whole * 2 * UNROLL, count % (2 * UNROLL))
 
     for n in range(2 * SWEEP):
         advance(fields[n % 2], fields[1 - n % 2], n + 1, span - 2 * n - 2,
@@ -353,8 +374,13 @@
     prepare = pl.pallas_call(
         prepare_kernel,
         out_shape=[tall] + [short] * 9,
-        in_specs=[vmem] * 4,
+        in_specs=[hbm] * 4,
         out_specs=[vmem] * 10,
+        scratch_shapes=[
+            pltpu.VMEM(perturb.shape, BF16),
+            pltpu.VMEM((3,) + k_north.shape, F32),
+            pltpu.SemaphoreType.DMA((7,)),
+        ],
         compiler_params=pltpu.CompilerParams(vmem_limit_bytes=44 * 2**20),
         cost_estimate=pl.CostEstimate(flops=0, bytes_accessed=24 * 2**20, transcendentals=0),
         name="prepare",

time: 81.9 us -> 80.9 us (0.988)
  Pallas kernels: 23.9 us -> 22.9 us
where the time goes in v5:
time: 80.9 us; the launch traced here: 80.5 us
  blocking collectives  25.7 us (32%)
  Pallas kernels  22.9 us (28%)
  waiting for transfers between devices  19.1 us (24%)
  starting transfers between devices  12 us (15%)
    ppermute x1, waiting for transfers between devices, shards(): below = lax.ppermute(last, 'lat', up)  17.6 us
    all_to_all x1, blocking collectives, shards(): mine = lax.all_to_all(spread, CHIP, 0, 0, tiled=True)  14.7 us
    pallas_call x1, Pallas kernels, shards(): pl.pallas_call(sweep_kernel, out_shape=[part, part] + [tall] + [short] *...  14.7 us
    all_to_all x1, blocking collectives, shards(): parts = lax.all_to_all(merged, CHIP, 0, 0, tiled=True)  11 us
    pallas_call x1, Pallas kernels, shards(): prepared = prepare(perturb, k_north, k_east, scale)  4.15 us
    ppermute x1, starting transfers between devices, shards(): high = lax.ppermute(bottom, 'lat', down)  4.03 us
    pallas_call x1, Pallas kernels, shards(): pl.pallas_call(edge_kernel, out_shape=[jax.ShapeDtypeStruct((rows, LANES)...  3.16 us
    ppermute x1, starting transfers between devices, shards(): above = lax.ppermute(first, 'lat', down)  2.67 us
  transfers between devices with their start and end apart: 6, of which 2 were waited for; matrix products, arithmetic and copies ran while one was open for 1% of the time, Pallas kernels for 5%

profile of v5, /device:TPU:1, one launch (start us, length us, event | category | flops | bytes accessed | tf_op | source)
XLA Modules:
  0.0 80.5 jit_solution(11733568463346664637)
XLA Ops:
  0.0 3.2 %edges.1 = (f32[32,128]{1,0:T(8,128)}, f32[8,128]{1,0:T(8,128)}, f32[8,128]{1,0:T(8,128)}, f32[28,8,1024]{2,1,0:T(8,128)}, f32[28,8,1024]{2,1,0:T(8,128)}) custom-call(f32[4,32,32]{2,1,0:T(8,128)} %gradient.1, bf16[4,4,32,1024]{3,2,1,0:T(8,128)(2,1)} %perturb_all.1, f32[4,32,1024]{2,1,0:T(8,128)} %north_all.1, f32[4,32,1024]{2,1,0:T(8,128)} %east_all.1, ...), custom_call_target="tpu_custom_call" | custom-call | tf_op jit(solution)/shard_map/edges/pallas_call | solution.py:346
  3.2 2.5 %collective-permute-start = (f32[28,8,1024]{2,1,0:T(8,128)}, f32[28,8,1024]{2,1,0:T(8,128)S(1)}, u32[]{:S(2)}, u32[]{:S(2)}) collective-permute-start(f32[28,8,1024]{2,1,0:T(8,128)} %get-tuple-element.22), channel_id=1, source_target_pairs={{0,1},{1,2},{2,3},{3,4},{4,5},{5,6},{6,7},{7,0},{8,9},{9,10},{10,1... | collective-permute-start | bytes 2752520 | tf_op jit(solution)/shard_map/ppermute | solution.py:362
  5.7 4.0 %collective-permute-start.1 = (f32[28,8,1024]{2,1,0:T(8,128)}, f32[28,8,1024]{2,1,0:T(8,128)}, u32[]{:S(2)}, u32[]{:S(2)}) collective-permute-start(f32[28,8,1024]{2,1,0:T(8,128)} %get-tuple-element.23), channel_id=1, source_target_pairs={{1,0},{2,1},{3,2},{4,3},{5,4},{6,5},{7,6},{0,7},{9,8},{10,9},{11,1... | collective-permute-start | bytes 2752520 | tf_op jit(solution)/shard_map/ppermute | solution.py:363
  9.7 0.0 collective-permute-start.2
  9.7 2.7 %collective-permute-start.3 = (f32[8,128]{1,0:T(8,128)}, f32[8,128]{1,0:T(8,128)S(1)}, u32[]{:S(2)}, u32[]{:S(2)}) collective-permute-start(f32[8,128]{1,0:T(8,128)} %get-tuple-element.26), channel_id=1, source_target_pairs={{1,0},{2,1},{3,2},{4,3},{5,4},{6,5},{7,6},{0,7},{9,8},{10,9},{11,1... | collective-permute-start | bytes 12296 | tf_op jit(solution)/shard_map/ppermute | solution.py:361
  12.4 17.6 %collective-permute-done.2 = f32[8,128]{1,0:T(8,128)S(1)} collective-permute-done((f32[8,128]{1,0:T(8,128)}, f32[8,128]{1,0:T(8,128)S(1)}, u32[]{:S(2)}, u32[]{:S(2)}) %collective-permute-start.2) | collective-permute-done | bytes 4128 | tf_op jit(solution)/shard_map/ppermute | solution.py:360
  30.0 0.0 collective-permute-done.3
  30.0 0.7 pad_maximum_fusion
  30.8 14.7 %all_to_all.10.mine = f32[16,48,128]{2,1,0:T(8,128)S(1)} all-to-all(f32[16,48,128]{2,1,0:T(8,128)S(1)} %broadcast_in_dim.2), channel_id=1, replica_groups=mesh['mem_0'=4,'mem_1'=4,'mem_2'=2,'lat'=8] {'mem_0','mem_1'}, dimensions={0} | all-to-all | bytes 786432 | tf_op jit(solution)/shard_map/all_to_all | solution.py:368
  45.4 2.6 %collective-permute-start.4 = (f32[16,48,128]{2,1,0:T(8,128)S(1)}, f32[16,48,128]{2,1,0:T(8,128)S(1)}, u32[]{:S(2)}, u32[]{:S(2)}) collective-permute-start(f32[16,48,128]{2,1,0:T(8,128)S(1)} %all_to_all.10.mine), channel_id=1, source_target_pairs={{0,8},{8,0},{1,9},{9,1},{2,10},{10,2},{3,11},{11,3},{4,12},{12,4},... | collective-permute-start | bytes 1179656 | tf_op jit(solution)/shard_map/ppermute | solution.py:369
  48.1 4.2 %prepare.1 = (f32[8,832,128]{2,1,0:T(8,128)S(1)}, f32[8,416,128]{2,1,0:T(8,128)S(1)}, f32[8,416,128]{2,1,0:T(8,128)S(1)}, f32[8,416,128]{2,1,0:T(8,128)S(1)}, f3...) custom-call(bf16[4,4,32,1024]{3,2,1,0:T(8,128)(2,1)} %perturb_all.1,, ...), custom_call_target="tpu_custom_call" | custom-call | bytes 25165824 | tf_op jit(solution)/shard_map/prepare/pallas_call | solution.py:388
  52.2 0.0 collective-permute-done.4.other
  52.3 0.0 collective-permute-done.low
  52.3 0.0 collective-permute-done.1.high
  52.3 14.7 %sweeps.1 = (f32[16,32,128]{2,1,0:T(8,128)S(1)}, f32[16,32,128]{2,1,0:T(8,128)S(1)}, f32[8,832,128]{2,1,0:T(8,128)S(1)}, f32[8,416,128]{2,1,0:T(8,128)S(1)}, f32...) custom-call(f32[28,8,1024]{2,1,0:T(8,128)S(1)} %collective-permute-d, ...), custom_call_target="tpu_custom_call", output_to_operand_aliasing={{2}: (4, {}), {3}: (5, {}), {4}: (6, {}), {5}: (7, {}), {6}... | custom-call | tf_op jit(solution)/shard_map/sweeps/pallas_call | solution.py:391
  67.0 0.1 collective-permute-start.5
  67.1 1.5 %collective-permute-done.5 = f32[16,32,128]{2,1,0:T(8,128)S(1)} collective-permute-done((f32[16,32,128]{2,1,0:T(8,128)S(1)}, f32[16,32,128]{2,1,0:T(8,128)S(1)}, u32[]{:S(2)}, u32[]{:S(2)}) %collective-permute-start.5) | collective-permute-done | bytes 262176 | tf_op jit(solution)/shard_map/ppermute | solution.py:409
  68.6 11.0 %all_to_all.11.p = f32[16,32,128]{2,1,0:T(8,128)S(1)} all-to-all(f32[16,32,128]{2,1,0:T(8,128)S(1)} %add.3), channel_id=1, replica_groups=mesh['mem_0'=4,'mem_1'=4,'mem_2'=2,'lat'=8] {'mem_0','mem_1'}, dimensions={0} | all-to-all | bytes 524288 | tf_op jit(solution)/shard_map/all_to_all | solution.py:410
  79.7 0.9 %finish.1 = f32[4,32,32]{2,1,0:T(8,128)} custom-call(f32[16,32,128]{2,1,0:T(8,128)S(1)} %all_to_all.11.p), custom_call_target="tpu_custom_call" | custom-call | tf_op jit(solution)/shard_map/finish/pallas_call | solution.py:412
  (2 shorter events, 0.1 us)
Async XLA Ops:
  3.2 49.1 %collective-permute-start = (f32[28,8,1024]{2,1,0:T(8,128)}, f32[28,8,1024]{2,1,0:T(8,128)S(1)}, u32[]{:S(2)}, u32[]{:S(2)}) collective-permute-start(f32[28,8,1024]{2,1,0:T(8,128)} %get-tuple-element.22), channel_id=1, source_target_pairs={{0,1},{1,2},{2,3},{3,4},{4,5},{5,6},{6,7},{7,0},{8,9},{9,10},{10,1... | collective-permute-start | bytes 2752520 | tf_op jit(solution)/shard_map/ppermute | solution.py:362
  5.7 46.6 %collective-permute-start.1 = (f32[28,8,1024]{2,1,0:T(8,128)}, f32[28,8,1024]{2,1,0:T(8,128)}, u32[]{:S(2)}, u32[]{:S(2)}) collective-permute-start(f32[28,8,1024]{2,1,0:T(8,128)} %get-tuple-element.23), channel_id=1, source_target_pairs={{1,0},{2,1},{3,2},{4,3},{5,4},{6,5},{7,6},{0,7},{9,8},{10,9},{11,1... | collective-permute-start | bytes 2752520 | tf_op jit(solution)/shard_map/ppermute | solution.py:363
  9.7 20.3 %collective-permute-start.2 = (f32[8,128]{1,0:T(8,128)}, f32[8,128]{1,0:T(8,128)S(1)}, u32[]{:S(2)}, u32[]{:S(2)}) collective-permute-start(f32[8,128]{1,0:T(8,128)} %get-tuple-element.24), channel_id=1, source_target_pairs={{0,1},{1,2},{2,3},{3,4},{4,5},{5,6},{6,7},{7,0},{8,9},{9,10},{10,1... | collective-permute-start | bytes 12296 | tf_op jit(solution)/shard_map/ppermute | solution.py:360
  9.7 20.3 %collective-permute-start.3 = (f32[8,128]{1,0:T(8,128)}, f32[8,128]{1,0:T(8,128)S(1)}, u32[]{:S(2)}, u32[]{:S(2)}) collective-permute-start(f32[8,128]{1,0:T(8,128)} %get-tuple-element.26), channel_id=1, source_target_pairs={{1,0},{2,1},{3,2},{4,3},{5,4},{6,5},{7,6},{0,7},{9,8},{10,9},{11,1... | collective-permute-start | bytes 12296 | tf_op jit(solution)/shard_map/ppermute | solution.py:361
  45.4 6.8 %collective-permute-start.4 = (f32[16,48,128]{2,1,0:T(8,128)S(1)}, f32[16,48,128]{2,1,0:T(8,128)S(1)}, u32[]{:S(2)}, u32[]{:S(2)}) collective-permute-start(f32[16,48,128]{2,1,0:T(8,128)S(1)} %all_to_all.10.mine), channel_id=1, source_target_pairs={{0,8},{8,0},{1,9},{9,1},{2,10},{10,2},{3,11},{11,3},{4,12},{12,4},... | collective-permute-start | bytes 1179656 | tf_op jit(solution)/shard_map/ppermute | solution.py:369
  67.0 1.6 %collective-permute-start.5 = (f32[16,32,128]{2,1,0:T(8,128)S(1)}, f32[16,32,128]{2,1,0:T(8,128)S(1)}, u32[]{:S(2)}, u32[]{:S(2)}) collective-permute-start(f32[16,32,128]{2,1,0:T(8,128)S(1)} %get-tuple-element.38), channel_id=1, source_target_pairs={{0,8},{8,0},{1,9},{9,1},{2,10},{10,2},{3,11},{11,3},{4,12},{12,4},... | collective-permute-start | bytes 786440 | tf_op jit(solution)/shard_map/ppermute | solution.py:409
